TPU v7x, 32 devices: a whole 2x2x4 slice. The times are simulated.
32 devices in a mesh: sensor: 16 (over z, x, core), day: 2 (over y).
Axes of the slice: x: 2, y: 2, z: 4, core: 2. Of those that a mesh axis runs over, the one named last changes fastest.
Arguments:
- traffic: bfloat16 [4096, 16384], P('sensor', 'day'), may hold values from -24 to 24
- start_basis: float32 [512, 64], replicated, may hold values from -6 to 6
Outputs:
- day_basis: float32 [512, 64], replicated
- core: bfloat16 [4096, 2048], P(('sensor', 'day'))
All inputs are finite; a program needn't handle non-finite values.
Results may differ from a plain program's by a relative error of at most 0.001.
The roundings to bfloat16 on the way count: a program that leaves them out, or rounds other values in their place, can miss the bound.
Values may be sent and summed in bfloat16 or wider, within the bound.
No kernel may reach another device: no remote copies, remote signals or barrier semaphores. Data moves between devices by JAX's collectives and lax.ppermute only.
A program may use at most 64 MiB of HBM per device.

v0:
```python
import jax
import jax.numpy as jnp
from jax import lax
from jax.sharding import PartitionSpec as P

ITERS = 3


def orthonormalize(images):
    product = jnp.dot(images.T, images, precision=lax.Precision.HIGHEST)
    lower = jnp.linalg.cholesky(product)
    return jax.scipy.linalg.solve_triangular(lower, images.T, lower=True).T


def shards(traffic, start_basis):
    regrouped = lax.all_to_all(traffic, "day", split_axis=0, concat_axis=1, tiled=True)
    sensors_here = regrouped.shape[0]
    days_all = start_basis.shape[0]
    components = regrouped.shape[1] // days_all
    series = regrouped.reshape(sensors_here, days_all, components)
    gram_local = lax.dot_general(
        series, series, (((0, 2), (0, 2)), ((), ())), preferred_element_type=jnp.float32
    )
    basis = start_basis
    gram = lax.psum(gram_local, ("sensor", "day"))
    for iteration in range(ITERS):
        basis = orthonormalize(jnp.dot(gram, basis, precision=lax.Precision.HIGHEST))
    day_basis = basis * jnp.sqrt(jnp.float32(days_all))
    basis_low = basis.astype(jnp.bfloat16)
    core = jnp.einsum("sdt,dr->str", series, basis_low, preferred_element_type=jnp.float32).astype(
        jnp.bfloat16
    )
    return (day_basis, core.reshape(sensors_here, components * basis_low.shape[1]))


def solution(mesh):
    placed = (P("sensor", "day"), P())
    return jax.shard_map(
        shards,
        mesh=mesh,
        in_specs=placed,
        out_specs=(P(), P(("sensor", "day"), None)),
        check_vma=False,
    )
```

profile of v0, /device:TPU:0, one launch (start us, length us, event | category | flops | bytes accessed | tf_op | source)
XLA Modules:
  0.0 272.0 jit_solution(9290917982691987709)
XLA Ops:
  7.2 56.3 %all_to_all.16 = bf16[2,128,8192]{2,1,0:T(8,128)(2,1)} all-to-all(bf16[2,128,8192]{2,1,0:T(8,128)(2,1)} %bitcast.66), channel_id=1, replica_groups=mesh['sensor'=16,'day'=2] {'day'}, dimensions={0} | all-to-all | bytes 8388608 | tf_op jit(solution)/shard_map/all_to_all | solution.py:16
  63.6 6.3 %copy.16 = bf16[128,2,8192]{0,2,1:T(8,128)(2,1)} copy(bf16[128,2,8192]{2,0,1:T(8,128)(2,1)} %bitcast.65) | data formatting | bytes 8388608 | tf_op jit(solution)/shard_map/all_to_all | solution.py:16
  69.9 7.6 %copy.18 = bf16[128,512,32]{1,0,2:T(8,128)(2,1)} copy(bf16[128,512,32]{0,2,1:T(8,128)(2,1)} %bitcast.64) | data formatting | bytes 8388608 | tf_op jit(solution)/shard_map/reshape | solution.py:20
  77.5 6.8 %convolution_bitcast_fusion = f32[512,512]{1,0:T(8,128)} fusion(bf16[128,512,32]{1,0,2:T(8,128)(2,1)} %copy.18), kind=kOutput, calls=%fused_computation | convolution fusion | flops 2147483648 | bytes 5242880 | tf_op jit(solution)/shard_map/dot_general | solution.py:21
  84.3 131.3 %all-reduce.2.cloned.1.call-done = f32[512,512]{1,0:T(8,128)} async-done(((f32[512,512]{1,0:T(8,128)}), f32[512,512]{1,0:T(8,128)}) %all-reduce.2.cloned.1.call-update) | async-done | bytes 1048592 | tf_op jit(solution)/shard_map/psum | solution.py:25
  215.6 2.4 fusion.21
  218.1 0.3 fusion.22
  218.3 0.1 copy.19
  218.4 5.8 %cholesky.59 = f32[64,64]{1,0:T(8,128)S(1)} custom-call(f32[64,64]{1,0:T(8,128)S(1)} %fusion.16), custom_call_target="Cholesky" | custom-call | tf_op jit(solution)/shard_map/jit(cholesky)/cholesky | solution.py:11
  224.3 0.6 compare_reduce_fusion.2
  225.0 0.7 fusion.8
  225.6 4.9 %custom-call.7 = f32[1,64,64]{1,2,0:T(8,128)S(1)} custom-call(f32[1,64,64]{2,1,0:T(8,128)S(1)} %fusion.8), custom_call_target="InvertDiagBlocksLowerTriangular" | custom-call | tf_op jit(solution)/shard_map/jit(_solve_triangular)/triangular_solve | solution.py:12
  230.5 0.3 fusion.4
  230.9 2.4 fusion.23
  233.2 0.3 fusion.24
  233.5 0.1 copy.20
  233.6 5.8 %cholesky.70 = f32[64,64]{1,0:T(8,128)S(1)} custom-call(f32[64,64]{1,0:T(8,128)S(1)} %fusion.14), custom_call_target="Cholesky" | custom-call | tf_op jit(solution)/shard_map/jit(cholesky)/cholesky | solution.py:11
  239.5 0.6 compare_reduce_fusion.1
  240.1 0.7 fusion.9
  240.8 4.9 %custom-call.8 = f32[1,64,64]{1,2,0:T(8,128)S(1)} custom-call(f32[1,64,64]{2,1,0:T(8,128)S(1)} %fusion.9), custom_call_target="InvertDiagBlocksLowerTriangular" | custom-call | tf_op jit(solution)/shard_map/jit(_solve_triangular)/triangular_solve | solution.py:12
  245.7 0.3 fusion.2
  246.0 1.1 fusion.25
  247.1 0.3 fusion.26
  247.4 0.1 copy.21
  247.5 5.8 %cholesky.81 = f32[64,64]{1,0:T(8,128)S(1)} custom-call(f32[64,64]{1,0:T(8,128)S(1)} %fusion.12), custom_call_target="Cholesky" | custom-call | tf_op jit(solution)/shard_map/jit(cholesky)/cholesky | solution.py:11
  253.4 0.6 compare_reduce_fusion
  254.0 0.7 fusion.10
  254.7 4.9 %custom-call.9 = f32[1,64,64]{1,2,0:T(8,128)S(1)} custom-call(f32[1,64,64]{2,1,0:T(8,128)S(1)} %fusion.10), custom_call_target="InvertDiagBlocksLowerTriangular" | custom-call | tf_op jit(solution)/shard_map/jit(_solve_triangular)/triangular_solve | solution.py:12
  259.6 0.3 fusion
  259.9 3.6 %convolution_convert_fusion = bf16[64,128,32]{1,0,2:T(8,128)(2,1)S(1)} fusion(bf16[128,512,32]{1,0,2:T(8,128)(2,1)} %copy.18, f32[64,512]{1,0:T(8,128)S(1)} %fusion), kind=kOutput, calls=%fused_computation.1 | convolution fusion | flops 268730368 | bytes 4849664 | tf_op jit(solution)/shard_map/sdt,dr->str/dot_general | solution.py:30
  263.5 0.7 multiply_bitcast_fusion
  264.2 1.0 copy.23
  (12 shorter events, 0.2 us)
Async XLA Ops:
  7.2 208.4 %copy-start = (f32[512,64]{0,1:T(8,128)S(1)}, f32[512,64]{0,1:T(8,128)}, u32[]{:S(2)}) copy-start(f32[512,64]{0,1:T(8,128)} %param.6) | copy-start | bytes 393220
  7.2 208.4 %all-reduce.2.cloned.1.call-start = ((), (), s32[]{:S(2)}) async-start(), calls=%async_computation.1 | async-start | bytes 2097152 | tf_op jit(solution)/shard_map/psum | solution.py:25
  215.6 30.4 %copy-start.1 = (f32[512,512]{1,0:T(8,128)S(1)}, f32[512,512]{1,0:T(8,128)}, u32[]{:S(2)}) copy-start(f32[512,512]{1,0:T(8,128)} %all-reduce.2.cloned.1.call-done) | copy-start | bytes 3145732
Sparse Core Ops, SparseCore 0:
  84.4 131.1 all-reduce.1
where the time goes:
time: 273 us; the launch traced here: 272 us
  waiting for transfers between devices  131 us (48%)
  blocking collectives  56.3 us (21%)
  other arithmetic  36.9 us (14%)
  matrix products  18.1 us (7%)
  local copies, waits for them, and re-layouts  15.1 us (6%)
  between operations  14.2 us (5%)
    psum x1, waiting for transfers between devices, shards(): gram = lax.psum(gram_local, ('sensor', 'day'))  131 us
    all_to_all x1, blocking collectives, shards(): lax.all_to_all(traffic, 'day', split_axis=0, concat_axis=1, tiled=True)  56.3 us
    another operation x9, other arithmetic, orthonormalize(): lower = jnp.linalg.cholesky(product)  19.6 us
    another operation x6, other arithmetic, orthonormalize(): return jax.scipy.linalg.solve_triangular(lower, images.T, lower=True).T  16.6 us
    reshape x1, local copies, waits for them, and re-layouts, shards(): series = regrouped.reshape(sensors_here, days_all, components)  7.55 us
    dot_general x1, matrix products, shards(): lax.dot_general(series, series, (((0, 2), (0, 2)), ((), ())), preferred_e...  6.83 us
    all_to_all x1, local copies, waits for them, and re-layouts, shards(): lax.all_to_all(traffic, 'day', split_axis=0, concat_axis=1, tiled=True)  6.35 us
    dot_general x3, matrix products, shards(): jnp.dot(gram, basis, precision=lax.Precision.HIGHEST)  5.94 us
  transfers between devices with their start and end apart: 1, of which 1 were waited for; matrix products, arithmetic and copies ran while one was open for 0% of the time, Pallas kernels for 0%

commit v1 on v0

--- a/solution.py
+++ b/solution.py
@@ -12,6 +12,15 @@
     return jax.scipy.linalg.solve_triangular(lower, images.T, lower=True).T
 
 
+def sum_over_devices(local, axes):
+    devices = lax.axis_size(axes)
+    pieces = local.reshape(devices, local.size // devices // 128, 128)
+    piece = jnp.sum(lax.all_to_all(pieces, axes, split_axis=0, concat_axis=0, tiled=True), axis=0)
+    copies = jnp.broadcast_to(piece, (devices, *piece.shape))
+    whole = lax.all_to_all(copies, axes, split_axis=0, concat_axis=0, tiled=True)
+    return whole.reshape(local.shape)
+
+
 def shards(traffic, start_basis):
     regrouped = lax.all_to_all(traffic, "day", split_axis=0, concat_axis=1, tiled=True)
     sensors_here = regrouped.shape[0]
@@ -22,7 +31,7 @@
         series, series, (((0, 2), (0, 2)), ((), ())), preferred_element_type=jnp.float32
     )
     basis = start_basis
-    gram = lax.psum(gram_local, ("sensor", "day"))
+    gram = sum_over_devices(gram_local, ("sensor", "day"))
     for iteration in range(ITERS):
         basis = orthonormalize(jnp.dot(gram, basis, precision=lax.Precision.HIGHEST))
     day_basis = basis * jnp.sqrt(jnp.float32(days_all))

time: 273 us -> 186 us (0.68)
  waiting for transfers between devices: 131 us -> 0 us
  blocking collectives: 56.3 us -> 117 us
  between operations: 14.2 us -> 0.79 us
  matrix products: 18.1 us -> 14.6 us
    psum x1 -> x0, waiting for transfers between devices: 131 us -> none  [shards(): gram = lax.psum(gram_local, ('sensor', 'day'))]
    all_to_all x0 -> x2, blocking collectives: none -> 60.7 us  [the longest x1 31.1 us: sum_over_devices(): lax.all_to_all(pieces, axes, split_axis=0, concat_axis=0, tiled=True)]
  transfers between devices with their start and end apart: 1 -> 0, of which waited for: 1 -> 0; matrix products, arithmetic and copies ran while one was open for 0% -> 0% of each run, Pallas kernels for 0% -> 0%
where the time goes in v1:
time: 186 us; the launch traced here: 185 us
  blocking collectives  117 us (63%)
  other arithmetic  37 us (20%)
  local copies, waits for them, and re-layouts  15.5 us (8%)
  matrix products  14.6 us (8%)
    all_to_all x1, blocking collectives, shards(): lax.all_to_all(traffic, 'day', split_axis=0, concat_axis=1, tiled=True)  56.5 us
    all_to_all x1, blocking collectives, sum_over_devices(): lax.all_to_all(pieces, axes, split_axis=0, concat_axis=0, tiled=True)  31.1 us
    all_to_all x1, blocking collectives, sum_over_devices(): lax.all_to_all(copies, axes, split_axis=0, concat_axis=0, tiled=True)  29.6 us
    another operation x9, other arithmetic, orthonormalize(): lower = jnp.linalg.cholesky(product)  19.6 us
    another operation x6, other arithmetic, orthonormalize(): return jax.scipy.linalg.solve_triangular(lower, images.T, lower=True).T  16.6 us
    reshape x1, local copies, waits for them, and re-layouts, shards(): series = regrouped.reshape(sensors_here, days_all, components)  7.57 us
    all_to_all x1, local copies, waits for them, and re-layouts, shards(): lax.all_to_all(traffic, 'day', split_axis=0, concat_axis=1, tiled=True)  6.36 us
    dot_general x1, matrix products, shards(): lax.dot_general(series, series, (((0, 2), (0, 2)), ((), ())), preferred_e...  5.81 us

profile of v1, /device:TPU:0, one launch (start us, length us, event | category | flops | bytes accessed | tf_op | source)
XLA Modules:
  0.0 185.1 jit_solution(1386019114363974592)
XLA Ops:
  0.6 56.5 %all_to_all.26 = bf16[2,128,8192]{2,1,0:T(8,128)(2,1)} all-to-all(bf16[2,128,8192]{2,1,0:T(8,128)(2,1)} %bitcast.66), channel_id=1, replica_groups=mesh['sensor'=16,'day'=2] {'day'}, dimensions={0} | all-to-all | bytes 8388608 | tf_op jit(solution)/shard_map/all_to_all | solution.py:25
  57.1 6.4 %copy.16 = bf16[128,2,8192]{0,2,1:T(8,128)(2,1)} copy(bf16[128,2,8192]{2,0,1:T(8,128)(2,1)} %bitcast.65) | data formatting | bytes 8388608 | tf_op jit(solution)/shard_map/all_to_all | solution.py:25
  63.5 7.6 %copy.18 = bf16[128,512,32]{1,0,2:T(8,128)(2,1)} copy(bf16[128,512,32]{0,2,1:T(8,128)(2,1)} %bitcast.64) | data formatting | bytes 8388608 | tf_op jit(solution)/shard_map/reshape | solution.py:29
  71.1 5.8 %convolution_bitcast_fusion = f32[512,512]{1,0:T(8,128)S(1)} fusion(bf16[128,512,32]{1,0,2:T(8,128)(2,1)} %copy.18), kind=kOutput, calls=%fused_computation | convolution fusion | flops 2147483648 | bytes 5242880 | tf_op jit(solution)/shard_map/dot_general | solution.py:30
  77.0 31.1 %all_to_all.27 = f32[32,64,128]{2,1,0:T(8,128)S(1)} all-to-all(f32[32,64,128]{2,1,0:T(8,128)S(1)} %reshape.29), channel_id=1, replica_groups=mesh['sensor'=16,'day'=2] {'sensor','day'}, dimensions={0} | all-to-all | bytes 2097152 | tf_op jit(solution)/shard_map/all_to_all | solution.py:18
  108.1 0.1 broadcast_in_dim.4
  108.3 29.6 %all_to_all.28 = f32[32,64,128]{2,1,0:T(8,128)S(1)} all-to-all(f32[32,64,128]{2,1,0:T(8,128)S(1)} %broadcast_in_dim.4), channel_id=1, replica_groups=mesh['sensor'=16,'day'=2] {'sensor','day'}, dimensions={0} | all-to-all | bytes 2097152 | tf_op jit(solution)/shard_map/all_to_all | solution.py:20
  137.9 0.2 reshape.30
  138.1 1.1 fusion.21
  139.2 0.3 fusion.22
  139.6 5.8 %cholesky.59 = f32[64,64]{1,0:T(8,128)S(1)} custom-call(f32[64,64]{1,0:T(8,128)S(1)} %fusion.16), custom_call_target="Cholesky" | custom-call | tf_op jit(solution)/shard_map/jit(cholesky)/cholesky | solution.py:11
  145.4 0.6 compare_reduce_fusion.2
  146.1 0.7 fusion.8
  146.7 4.9 %custom-call.7 = f32[1,64,64]{1,2,0:T(8,128)S(1)} custom-call(f32[1,64,64]{2,1,0:T(8,128)S(1)} %fusion.8), custom_call_target="InvertDiagBlocksLowerTriangular" | custom-call | tf_op jit(solution)/shard_map/jit(_solve_triangular)/triangular_solve | solution.py:12
  151.6 0.3 fusion.4
  152.0 1.1 fusion.23
  153.1 0.3 fusion.24
  153.5 5.8 %cholesky.70 = f32[64,64]{1,0:T(8,128)S(1)} custom-call(f32[64,64]{1,0:T(8,128)S(1)} %fusion.14), custom_call_target="Cholesky" | custom-call | tf_op jit(solution)/shard_map/jit(cholesky)/cholesky | solution.py:11
  159.4 0.6 compare_reduce_fusion.1
  160.0 0.7 fusion.9
  160.7 4.9 %custom-call.8 = f32[1,64,64]{1,2,0:T(8,128)S(1)} custom-call(f32[1,64,64]{2,1,0:T(8,128)S(1)} %fusion.9), custom_call_target="InvertDiagBlocksLowerTriangular" | custom-call | tf_op jit(solution)/shard_map/jit(_solve_triangular)/triangular_solve | solution.py:12
  165.6 0.3 fusion.2
  165.9 1.1 fusion.25
  167.1 0.3 fusion.26
  167.4 5.8 %cholesky.81 = f32[64,64]{1,0:T(8,128)S(1)} custom-call(f32[64,64]{1,0:T(8,128)S(1)} %fusion.12), custom_call_target="Cholesky" | custom-call | tf_op jit(solution)/shard_map/jit(cholesky)/cholesky | solution.py:11
  173.3 0.6 compare_reduce_fusion
  173.9 0.7 fusion.10
  174.6 4.9 %custom-call.9 = f32[1,64,64]{1,2,0:T(8,128)S(1)} custom-call(f32[1,64,64]{2,1,0:T(8,128)S(1)} %fusion.10), custom_call_target="InvertDiagBlocksLowerTriangular" | custom-call | tf_op jit(solution)/shard_map/jit(_solve_triangular)/triangular_solve | solution.py:12
  179.5 0.3 fusion
  179.8 3.6 %convolution_convert_fusion = bf16[64,128,32]{1,0,2:T(8,128)(2,1)S(1)} fusion(bf16[128,512,32]{1,0,2:T(8,128)(2,1)} %copy.18, f32[64,512]{1,0:T(8,128)S(1)} %fusion), kind=kOutput, calls=%fused_computation.1 | convolution fusion | flops 268730368 | bytes 4849664 | tf_op jit(solution)/shard_map/sdt,dr->str/dot_general | solution.py:39
  183.4 0.7 multiply_bitcast_fusion
  184.1 1.0 copy.23
  (13 shorter events, 0.5 us)
Async XLA Ops:
  0.6 137.4 %copy-start = (f32[512,64]{0,1:T(8,128)S(1)}, f32[512,64]{0,1:T(8,128)}, u32[]{:S(2)}) copy-start(f32[512,64]{0,1:T(8,128)} %param.6) | copy-start | bytes 393220

commit v2 on v1

v2 whole, which is shorter than its diff:
```python
import functools

import jax
import jax.numpy as jnp
from jax import lax
from jax.experimental import pallas as pl
from jax.experimental.pallas import tpu as pltpu
from jax.sharding import PartitionSpec as P

ITERS = 3
AXES = ("sensor", "day")


def dot32(left, right, dims):
    return lax.dot_general(
        left,
        right,
        (dims, ((), ())),
        precision=lax.Precision.HIGHEST,
        preferred_element_type=jnp.float32,
    )


def inverse_factor(product, width=8):
    rank = product.shape[0]
    rows_at = lax.broadcasted_iota(jnp.int32, (rank, rank), 0)
    lanes_at = lax.broadcasted_iota(jnp.int32, (rank, rank), 1)
    unit = jnp.where(rows_at == lanes_at, 1.0, 0.0).astype(jnp.float32)
    both = jnp.concatenate([product, unit], axis=1)
    panels = [both[at : at + width] for at in range(0, rank, width)]
    row_of = lax.broadcasted_iota(jnp.int32, (width, 2 * rank), 0)

    def spread(values):
        return jnp.broadcast_to(values, (width, 2 * rank))

    done = []
    for here in range(rank // width):
        base = here * width
        below = range(here + 1, rank // width)
        rows = [spread(panels[here][w : w + 1]) for w in range(width)]
        pivots = {
            (v, w): spread(rows[v][:, base + w : base + w + 1])
            for v in range(width)
            for w in range(v, width)
        }
        columns = {
            (i, w): spread(panels[i][:, base + w : base + w + 1])
            for i in below
            for w in range(width)
        }
        for v in range(width):
            scale = lax.rsqrt(pivots[v, v])
            rows[v] = rows[v] * scale
            for w in range(v + 1, width):
                pivots[v, w] = pivots[v, w] * scale
            for i in below:
                columns[i, v] = columns[i, v] * scale
            for w in range(v + 1, width):
                for x in range(w, width):
                    pivots[w, x] = pivots[w, x] - pivots[v, w] * pivots[v, x]
                rows[w] = rows[w] - pivots[v, w] * rows[v]
                for i in below:
                    columns[i, w] = columns[i, w] - pivots[v, w] * columns[i, v]
            for i in below:
                panels[i] = panels[i] - columns[i, v] * rows[v]
        panel = rows[0]
        for w in range(1, width):
            panel = jnp.where(row_of == w, rows[w], panel)
        done.append(panel)
    return jnp.concatenate(done, axis=0)[:, rank:]


def rounds_kernel(gram_ref, start_ref, day_basis_ref, low_ref):
    def one_round(_, basis):
        images = dot32(basis, gram_ref[...], ((1,), (0,)))
        product = dot32(images, images, ((1,), (1,)))
        return dot32(inverse_factor(product), images, ((1,), (0,)))

    basis = lax.fori_loop(0, ITERS, one_round, start_ref[...])
    day_basis_ref[...] = basis * jnp.sqrt(jnp.float32(basis.shape[1]))
    low_ref[...] = basis.astype(jnp.bfloat16)


def rounds(gram, start):
    rank, days = start.shape
    whole = pl.BlockSpec(memory_space=pltpu.VMEM)
    return pl.pallas_call(
        rounds_kernel,
        out_shape=(
            jax.ShapeDtypeStruct((rank, days), jnp.float32),
            jax.ShapeDtypeStruct((rank, days), jnp.bfloat16),
        ),
        in_specs=[whole, whole],
        out_specs=(whole, whole),
        name="rounds",
    )(gram, start)


def sum_over_devices(local, axes):
    devices = lax.axis_size(axes)
    pieces = local.reshape(devices, local.size // devices // 128, 128)
    piece = jnp.sum(lax.all_to_all(pieces, axes, split_axis=0, concat_axis=0, tiled=True), axis=0)
    copies = jnp.broadcast_to(piece, (devices, *piece.shape))
    whole = lax.all_to_all(copies, axes, split_axis=0, concat_axis=0, tiled=True)
    return whole.reshape(local.shape)


def shards(traffic, start_basis):
    regrouped = lax.all_to_all(traffic, "day", split_axis=0, concat_axis=1, tiled=True)
    sensors_here = regrouped.shape[0]
    days_all = start_basis.shape[0]
    components = regrouped.shape[1] // days_all
    series = regrouped.reshape(sensors_here, days_all, components)
    gram_local = lax.dot_general(
        series, series, (((0, 2), (0, 2)), ((), ())), preferred_element_type=jnp.float32
    )
    gram = sum_over_devices(gram_local, AXES)
    day_basis, basis_low = rounds(gram, start_basis.T)
    core = jnp.einsum("sdt,rd->str", series, basis_low, preferred_element_type=jnp.float32).astype(
        jnp.bfloat16
    )
    return (day_basis.T, core.reshape(sensors_here, components * basis_low.shape[0]))


def solution(mesh):
    placed = (P("sensor", "day"), P())
    return jax.shard_map(
        shards,
        mesh=mesh,
        in_specs=placed,
        out_specs=(P(), P(AXES, None)),
        check_vma=False,
    )
```

time: 186 us -> 156 us (0.84)
  other arithmetic: 37 us -> 0.07 us
  Pallas kernels: 0 us -> 11.7 us
  matrix products: 14.6 us -> 9.42 us
    another operation x15 -> x0, other arithmetic: 36.2 us -> none  [the longest x9 19.6 us: orthonormalize(): lower = jnp.linalg.cholesky(product)]
    pallas_call x0 -> x1, Pallas kernels: none -> 11.7 us  [rounds(): pl.pallas_call(rounds_kernel, out_shape=(jax.ShapeDtypeStruct((rank, days...]
    dot_general x7 -> x1, matrix products: 7.76 us -> 3.6 us  [shards(): jnp.einsum('sdt,rd->str', series, basis_low, preferred_element_type=jnp.f...]
where the time goes in v2:
time: 156 us; the launch traced here: 155 us
  blocking collectives  117 us (75%)
  local copies, waits for them, and re-layouts  16.2 us (10%)
  Pallas kernels  11.7 us (8%)
  matrix products  9.42 us (6%)
    all_to_all x1, blocking collectives, shards(): lax.all_to_all(traffic, 'day', split_axis=0, concat_axis=1, tiled=True)  56.3 us
    all_to_all x1, blocking collectives, sum_over_devices(): lax.all_to_all(pieces, axes, split_axis=0, concat_axis=0, tiled=True)  31.1 us
    all_to_all x1, blocking collectives, sum_over_devices(): lax.all_to_all(copies, axes, split_axis=0, concat_axis=0, tiled=True)  29.6 us
    pallas_call x1, Pallas kernels, rounds(): pl.pallas_call(rounds_kernel, out_shape=(jax.ShapeDtypeStruct((rank, days...  11.7 us
    reshape x1, local copies, waits for them, and re-layouts, shards(): series = regrouped.reshape(sensors_here, days_all, components)  7.55 us
    all_to_all x1, local copies, waits for them, and re-layouts, shards(): lax.all_to_all(traffic, 'day', split_axis=0, concat_axis=1, tiled=True)  6.35 us
    dot_general x1, matrix products, shards(): lax.dot_general(series, series, (((0, 2), (0, 2)), ((), ())), preferred_e...  5.81 us
    dot_general x1, matrix products, shards(): jnp.einsum('sdt,rd->str', series, basis_low, preferred_element_type=jnp.f...  3.6 us

profile of v2, /device:TPU:0, one launch (start us, length us, event | category | flops | bytes accessed | tf_op | source)
XLA Modules:
  0.0 155.1 jit_solution(9409438814728571101)
XLA Ops:
  0.6 56.3 %all_to_all.26 = bf16[2,128,8192]{2,1,0:T(8,128)(2,1)} all-to-all(bf16[2,128,8192]{2,1,0:T(8,128)(2,1)} %bitcast.18), channel_id=1, replica_groups=mesh['sensor'=16,'day'=2] {'day'}, dimensions={0} | all-to-all | bytes 8388608 | tf_op jit(solution)/shard_map/all_to_all | solution.py:109
  57.0 6.3 %copy.10 = bf16[128,2,8192]{0,2,1:T(8,128)(2,1)} copy(bf16[128,2,8192]{2,0,1:T(8,128)(2,1)} %bitcast.17) | data formatting | bytes 8388608 | tf_op jit(solution)/shard_map/all_to_all | solution.py:109
  63.3 7.6 %copy.12 = bf16[128,512,32]{1,0,2:T(8,128)(2,1)} copy(bf16[128,512,32]{0,2,1:T(8,128)(2,1)} %bitcast.16) | data formatting | bytes 8388608 | tf_op jit(solution)/shard_map/reshape | solution.py:113
  70.9 5.8 %convolution_bitcast_fusion = f32[512,512]{1,0:T(8,128)S(1)} fusion(bf16[128,512,32]{1,0,2:T(8,128)(2,1)} %copy.12), kind=kOutput, calls=%fused_computation | convolution fusion | flops 2147483648 | bytes 5242880 | tf_op jit(solution)/shard_map/dot_general | solution.py:114
  76.7 0.1 reshape.21
  76.8 31.1 %all_to_all.27 = f32[32,64,128]{2,1,0:T(8,128)S(1)} all-to-all(f32[32,64,128]{2,1,0:T(8,128)S(1)} %reshape.21), channel_id=1, replica_groups=mesh['sensor'=16,'day'=2] {'sensor','day'}, dimensions={0} | all-to-all | bytes 2097152 | tf_op jit(solution)/shard_map/all_to_all | solution.py:102
  107.9 0.1 reduce_sum.9
  107.9 0.1 broadcast_in_dim.3
  108.1 29.6 %all_to_all.28 = f32[32,64,128]{2,1,0:T(8,128)S(1)} all-to-all(f32[32,64,128]{2,1,0:T(8,128)S(1)} %broadcast_in_dim.3), channel_id=1, replica_groups=mesh['sensor'=16,'day'=2] {'sensor','day'}, dimensions={0} | all-to-all | bytes 2097152 | tf_op jit(solution)/shard_map/all_to_all | solution.py:104
  137.7 1.1 reshape.22.gram_ref
  138.8 11.7 %rounds.1 = (f32[64,512]{1,0:T(8,128)}, bf16[64,512]{1,0:T(8,128)(2,1)}) custom-call(f32[512,512]{1,0:T(8,128)} %reshape.22.gram_ref, f32[64,512]{1,0:T(8,128)} %bitcast.20), custom_call_target="tpu_custom_call" | custom-call | tf_op jit(solution)/shard_map/rounds/pallas_call | solution.py:87
  150.5 3.6 %convolution_convert_fusion = bf16[64,128,32]{1,0,2:T(8,128)(2,1)S(1)} fusion(bf16[128,512,32]{1,0,2:T(8,128)(2,1)} %copy.12, bf16[64,512]{1,0:T(8,128)(2,1)} %get-tuple-element.5), kind=kOutput, calls=%fused_computation.1 | convolution fusion | flops 268697600 | bytes 4784128 | tf_op jit(solution)/shard_map/sdt,rd->str/dot_general | solution.py:119
  154.1 1.0 copy.14

commit v3 on v2

--- a/solution.py
+++ b/solution.py
@@ -70,39 +70,262 @@
     return jnp.concatenate(done, axis=0)[:, rank:]
 
 
-def rounds_kernel(gram_ref, start_ref, day_basis_ref, low_ref):
-    def one_round(_, basis):
-        images = dot32(basis, gram_ref[...], ((1,), (0,)))
-        product = dot32(images, images, ((1,), (1,)))
-        return dot32(inverse_factor(product), images, ((1,), (0,)))
-
-    basis = lax.fori_loop(0, ITERS, one_round, start_ref[...])
+def one_round(gram_ref, basis):
+    images = dot32(basis, gram_ref[...], ((1,), (0,)))
+    product = dot32(images, images, ((1,), (1,)))
+    return dot32(inverse_factor(product), images, ((1,), (0,)))
+
+
+def finish(basis, day_basis_ref, low_ref):
     day_basis_ref[...] = basis * jnp.sqrt(jnp.float32(basis.shape[1]))
     low_ref[...] = basis.astype(jnp.bfloat16)
 
 
+def rounds_kernel(gram_ref, start_ref, day_basis_ref, low_ref):
+    basis = lax.fori_loop(0, ITERS, lambda _, b: one_round(gram_ref, b), start_ref[...])
+    finish(basis, day_basis_ref, low_ref)
+
+
+def pieces_rounds_kernel(sensor, own, pieces_ref, start_ref, day_basis_ref, low_ref, gram_ref):
+    half = gram_ref.shape[0] // 2
+    side = half // 2
+    for day in range(2):
+        packed = jnp.concatenate([pieces_ref[2 * s + day, :own] for s in range(sensor)], axis=0)
+        first, cross, second = packed[:side], packed[side : 2 * side], packed[2 * side :]
+        at = day * half
+        gram_ref[at : at + side, at : at + side] = first
+        gram_ref[at + side : at + half, at : at + side] = cross
+        gram_ref[at : at + side, at + side : at + half] = cross.T
+        gram_ref[at + side : at + half, at + side : at + half] = second
+    off = jnp.concatenate([pieces_ref[d, own:] for d in range(2 * sensor)], axis=0)
+    for part in range(2):
+        block = off[part * half : (part + 1) * half]
+        gram_ref[:half, half + part * side : half + (part + 1) * side] = block
+        gram_ref[half + part * side : half + (part + 1) * side, :half] = block.T
+    basis = lax.fori_loop(0, ITERS, lambda _, b: one_round(gram_ref, b), start_ref[...])
+    finish(basis, day_basis_ref, low_ref)
+
+
+WHOLE = pl.BlockSpec(memory_space=pltpu.VMEM)
+VMEM_LIMIT = 24 * 1024 * 1024
+
+
+def basis_shapes(start):
+    return (
+        jax.ShapeDtypeStruct(start.shape, jnp.float32),
+        jax.ShapeDtypeStruct(start.shape, jnp.bfloat16),
+    )
+
+
 def rounds(gram, start):
-    rank, days = start.shape
-    whole = pl.BlockSpec(memory_space=pltpu.VMEM)
     return pl.pallas_call(
         rounds_kernel,
-        out_shape=(
-            jax.ShapeDtypeStruct((rank, days), jnp.float32),
-            jax.ShapeDtypeStruct((rank, days), jnp.bfloat16),
-        ),
-        in_specs=[whole, whole],
-        out_specs=(whole, whole),
+        out_shape=basis_shapes(start),
+        in_specs=[WHOLE, WHOLE],
+        out_specs=(WHOLE, WHOLE),
         name="rounds",
     )(gram, start)
 
 
+def pieces_rounds(pieces, own, start):
+    days = start.shape[1]
+    return pl.pallas_call(
+        functools.partial(pieces_rounds_kernel, pieces.shape[0] // 2, own),
+        out_shape=basis_shapes(start),
+        in_specs=[WHOLE, WHOLE],
+        out_specs=(WHOLE, WHOLE),
+        scratch_shapes=[pltpu.VMEM((days, days), jnp.float32)],
+        compiler_params=pltpu.CompilerParams(vmem_limit_bytes=VMEM_LIMIT),
+        name="rounds",
+    )(pieces, start)
+
+
+GROUP = 8
+
+
+def components_first(traffic, components, put):
+    width = GROUP * components
+    sensors = traffic.shape[0]
+    row = lax.broadcasted_iota(jnp.int32, (width, width), 0)
+    lane = lax.broadcasted_iota(jnp.int32, (width, width), 1)
+    order = (row % GROUP) * components + row // GROUP == lane
+    order = jnp.where(order, 1.0, 0.0).astype(jnp.bfloat16)
+    for pair in range(traffic.shape[1] // (2 * width)):
+        parts = []
+        for at in (2 * pair * width, (2 * pair + 1) * width):
+            turned = lax.dot_general(
+                order,
+                traffic[:, at : at + width],
+                (((1,), (1,)), ((), ())),
+                preferred_element_type=jnp.float32,
+            )
+            parts.append(turned.reshape(components, GROUP, sensors))
+        put(2 * GROUP * pair, jnp.concatenate(parts, axis=1).astype(jnp.bfloat16))
+
+
+def paired_dot(left_ref, right_ref):
+    components, _, sensors = left_ref.shape
+    step = max(1, 256 // sensors)
+    total = None
+    for at in range(0, components, step):
+        left, right = (
+            jnp.concatenate([ref[c] for c in range(at, at + step)], axis=1)
+            for ref in (left_ref, right_ref)
+        )
+        term = lax.dot_general(
+            left, right, (((1,), (1,)), ((), ())), preferred_element_type=jnp.float32
+        )
+        total = term if total is None else total + term
+    return total
+
+
+def local_kernel(traffic_ref, series_ref, packed_ref):
+    components = series_ref.shape[0]
+
+    def put(day, values):
+        series_ref[:, day : day + values.shape[1], :] = values
+
+    components_first(traffic_ref, components, put)
+    gram = paired_dot(series_ref, series_ref)
+    side = gram.shape[0] // 2
+    packed_ref[:side] = gram[:side, :side]
+    packed_ref[side : 2 * side] = gram[side:, :side]
+    packed_ref[2 * side :] = gram[side:, side:]
+
+
+def local(traffic, days, components):
+    sensors = traffic.shape[0]
+    side = days // 2
+    return pl.pallas_call(
+        local_kernel,
+        out_shape=(
+            jax.ShapeDtypeStruct((components, days, sensors), jnp.bfloat16),
+            jax.ShapeDtypeStruct((3 * side, side), jnp.float32),
+        ),
+        in_specs=[WHOLE],
+        out_specs=(WHOLE, WHOLE),
+        compiler_params=pltpu.CompilerParams(vmem_limit_bytes=VMEM_LIMIT),
+        cost_estimate=pl.CostEstimate(
+            flops=2 * traffic.size * (days + 256), bytes_accessed=4 * traffic.size, transcendentals=0
+        ),
+        name="local",
+    )(traffic)
+
+
+def arrived_kernel(before, day_ref, traffic_ref, series_ref, *refs):
+    parts, (arrived_ref, gram_ref) = refs[:before], refs[before:]
+
+    def put(day, values):
+        arrived_ref[:, day : day + values.shape[1], :] = values
+
+    components_first(traffic_ref, series_ref.shape[0], put)
+    gram = paired_dot(arrived_ref, series_ref)
+    if gram_ref.shape == gram.shape:
+        gram_ref[...] = gram
+        return
+    gram = jnp.concatenate([*(part[...] for part in parts), gram], axis=0)
+    side = gram_ref.shape[1]
+
+    @pl.when(day_ref[0] == 0)
+    def _():
+        turned = gram.T
+        gram_ref[: turned.shape[0]] = turned[:, :side]
+        gram_ref[turned.shape[0] :] = turned[:, side:]
+
+    @pl.when(day_ref[0] != 0)
+    def _():
+        gram_ref[: gram.shape[0]] = gram[:, :side]
+        gram_ref[gram.shape[0] :] = gram[:, side:]
+
+
+def arrived(day, traffic, series, parts, last):
+    components, days, _ = series.shape
+    sensors = traffic.shape[0]
+    here = traffic.shape[1] // components
+    gram_shape = (2 * days, days // 2) if last else (here, days)
+    grid_spec = pltpu.PrefetchScalarGridSpec(
+        num_scalar_prefetch=1,
+        grid=(1,),
+        in_specs=[
+            pl.BlockSpec(traffic.shape, lambda i, day: (0, 0)),
+            pl.BlockSpec((components, days, sensors), lambda i, day: (0, 0, day[0])),
+            *(pl.BlockSpec(part.shape, lambda i, day: (0, 0)) for part in parts),
+        ],
+        out_specs=(
+            pl.BlockSpec((components, here, sensors), lambda i, day: (0, 0, 0)),
+            pl.BlockSpec(gram_shape, lambda i, day: (0, 0)),
+        ),
+    )
+    return pl.pallas_call(
+        functools.partial(arrived_kernel, len(parts)),
+        grid_spec=grid_spec,
+        out_shape=(
+            jax.ShapeDtypeStruct((components, here, sensors), jnp.bfloat16),
+            jax.ShapeDtypeStruct(gram_shape, jnp.float32),
+        ),
+        compiler_params=pltpu.CompilerParams(vmem_limit_bytes=VMEM_LIMIT),
+        cost_estimate=pl.CostEstimate(
+            flops=2 * traffic.size * (days + 256), bytes_accessed=4 * traffic.size, transcendentals=0
+        ),
+        name="arrived",
+    )(day, traffic, series, *parts)
+
+
+def project_kernel(day_ref, own_basis_ref, other_basis_ref, series_ref, *refs):
+    arrived_refs, core_ref = refs[:-1], refs[-1]
+    components = series_ref.shape[0]
+    rank = own_basis_ref.shape[0]
+
+    def column(c):
+        other = jnp.concatenate([ref[c] for ref in arrived_refs], axis=0)
+        values = jnp.dot(own_basis_ref[...], series_ref[c], preferred_element_type=jnp.float32)
+        values += jnp.dot(other_basis_ref[...], other, preferred_element_type=jnp.float32)
+        return values
+
+    step = 128 // rank
+    for c in range(0, components, step):
+        values = jnp.concatenate([column(c + k) for k in range(step)], axis=0)
+        core_ref[:, c * rank : (c + step) * rank] = values.T.astype(jnp.bfloat16)
+
+
+def project(day, basis, series, parts):
+    components, days, _ = series.shape
+    sensors = parts[0].shape[2]
+    rank = basis.shape[0]
+    grid_spec = pltpu.PrefetchScalarGridSpec(
+        num_scalar_prefetch=1,
+        grid=(1,),
+        in_specs=[
+            pl.BlockSpec((rank, days), lambda i, day: (0, day[0])),
+            pl.BlockSpec((rank, days), lambda i, day: (0, 1 - day[0])),
+            pl.BlockSpec((components, days, sensors), lambda i, day: (0, 0, day[0])),
+            *(pl.BlockSpec(part.shape, lambda i, day: (0, 0, 0)) for part in parts),
+        ],
+        out_specs=pl.BlockSpec((sensors, components * rank), lambda i, day: (0, 0)),
+    )
+    return pl.pallas_call(
+        project_kernel,
+        grid_spec=grid_spec,
+        out_shape=jax.ShapeDtypeStruct((sensors, components * rank), jnp.bfloat16),
+        compiler_params=pltpu.CompilerParams(vmem_limit_bytes=VMEM_LIMIT),
+        name="project",
+    )(day, basis, basis, series, *parts)
+
+
+def scatter_sum(values, axes):
+    devices = lax.axis_size(axes)
+    pieces = values.reshape(devices, values.shape[0] // devices, values.shape[1])
+    return jnp.sum(lax.all_to_all(pieces, axes, split_axis=0, concat_axis=0, tiled=True), axis=0)
+
+
+def gather(piece, axes):
+    copies = jnp.broadcast_to(piece, (lax.axis_size(axes), *piece.shape))
+    return lax.all_to_all(copies, axes, split_axis=0, concat_axis=0, tiled=True)
+
+
 def sum_over_devices(local, axes):
-    devices = lax.axis_size(axes)
-    pieces = local.reshape(devices, local.size // devices // 128, 128)
-    piece = jnp.sum(lax.all_to_all(pieces, axes, split_axis=0, concat_axis=0, tiled=True), axis=0)
-    copies = jnp.broadcast_to(piece, (devices, *piece.shape))
-    whole = lax.all_to_all(copies, axes, split_axis=0, concat_axis=0, tiled=True)
-    return whole.reshape(local.shape)
+    flat = local.reshape(local.size // 128, 128)
+    return gather(scatter_sum(flat, axes), axes).reshape(local.shape)
 
 
 def shards(traffic, start_basis):
@@ -122,10 +345,42 @@
     return (day_basis.T, core.reshape(sensors_here, components * basis_low.shape[0]))
 
 
+CHUNKS = 4
+
+
+def paired_shards(traffic, start_basis):
+    days = start_basis.shape[0] // 2
+    components = traffic.shape[1] // days
+    sensors = traffic.shape[0] // 2
+    day = lax.axis_index("day")
+    swap = [(0, 1), (1, 0)]
+    wanted = lax.dynamic_slice_in_dim(traffic, (1 - day) * sensors, sensors, axis=0)
+    chunks = [
+        lax.ppermute(chunk, "day", swap) for chunk in jnp.split(wanted, CHUNKS, axis=1)
+    ]
+    series, packed = local(traffic, days, components)
+    own = scatter_sum(packed, "sensor")
+    index = day.astype(jnp.int32).reshape(1)
+    parts, grams = [], []
+    for at, chunk in enumerate(chunks):
+        last = at == CHUNKS - 1
+        part, gram = arrived(index, chunk, series, grams if last else (), last)
+        parts.append(part)
+        grams.append(gram)
+    off = scatter_sum(grams[-1], AXES)
+    pieces = gather(jnp.concatenate([own, off], axis=0), AXES)
+    day_basis, basis_low = pieces_rounds(pieces, own.shape[0], start_basis.T)
+    return (day_basis.T, project(index, basis_low, series, parts))
+
+
+def pairs(mesh):
+    return mesh.shape["day"] == 2
+
+
 def solution(mesh):
     placed = (P("sensor", "day"), P())
     return jax.shard_map(
-        shards,
+        paired_shards if pairs(mesh) else shards,
         mesh=mesh,
         in_specs=placed,
         out_specs=(P(), P(AXES, None)),

time: 156 us -> 107 us (0.69)
  blocking collectives: 117 us -> 19.9 us
  waiting for transfers between devices: 0 us -> 34.1 us
  starting transfers between devices: 0 us -> 17.4 us
  Pallas kernels: 11.7 us -> 24.4 us
  matrix products: 9.42 us -> 0 us
  local copies, waits for them, and re-layouts: 16.2 us -> 9.21 us
    all_to_all x3 -> x1, blocking collectives: 117 us -> 19.9 us  [gather(): return lax.all_to_all(copies, axes, split_axis=0, concat_axis=0, tiled=True)]
    ppermute x0 -> x4, waiting for transfers between devices: none -> 23.4 us  [paired_shards(): lax.ppermute(chunk, 'day', swap)]
    pallas_call x1 -> x7, Pallas kernels: 11.7 us -> 24.4 us  [the longest x1 10.6 us: pieces_rounds(): pl.pallas_call(functools.partial(pieces_rounds_kernel, pieces.shape[0] //...]
    all_to_all x0 -> x2, starting transfers between devices: none -> 12.4 us  [scatter_sum(): lax.all_to_all(pieces, axes, split_axis=0, concat_axis=0, tiled=True)]
    all_to_all x0 -> x2, waiting for transfers between devices: none -> 10.6 us  [scatter_sum(): lax.all_to_all(pieces, axes, split_axis=0, concat_axis=0, tiled=True)]
    dot_general x2 -> x0, matrix products: 9.42 us -> none  [the longest x1 5.81 us: shards(): lax.dot_general(series, series, (((0, 2), (0, 2)), ((), ())), preferred_e...]
    reshape x3 -> x0, local copies, waits for them, and re-layouts: 8.76 us -> none  [the longest x1 7.55 us: shards(): series = regrouped.reshape(sensors_here, days_all, components)]
    all_to_all x1 -> x0, local copies, waits for them, and re-layouts: 6.35 us -> none  [shards(): lax.all_to_all(traffic, 'day', split_axis=0, concat_axis=1, tiled=True)]
  transfers between devices with their start and end apart: 0 -> 6, of which waited for: 0 -> 4; matrix products, arithmetic and copies ran while one was open for 0% -> 0% of each run, Pallas kernels for 0% -> 11%
where the time goes in v3:
time: 107 us; the launch traced here: 106 us
  waiting for transfers between devices  34.1 us (32%)
  Pallas kernels  24.4 us (23%)
  blocking collectives  19.9 us (19%)
  starting transfers between devices  17.4 us (16%)
  local copies, waits for them, and re-layouts  9.21 us (9%)
    ppermute x4, waiting for transfers between devices, paired_shards(): lax.ppermute(chunk, 'day', swap)  23.4 us
    all_to_all x1, blocking collectives, gather(): return lax.all_to_all(copies, axes, split_axis=0, concat_axis=0, tiled=True)  19.9 us
    all_to_all x2, starting transfers between devices, scatter_sum(): lax.all_to_all(pieces, axes, split_axis=0, concat_axis=0, tiled=True)  12.4 us
    pallas_call x1, Pallas kernels, pieces_rounds(): pl.pallas_call(functools.partial(pieces_rounds_kernel, pieces.shape[0] //...  10.6 us
    all_to_all x2, waiting for transfers between devices, scatter_sum(): lax.all_to_all(pieces, axes, split_axis=0, concat_axis=0, tiled=True)  10.6 us
    pallas_call x4, Pallas kernels, arrived(): pl.pallas_call(functools.partial(arrived_kernel, len(parts)), grid_spec=g...  6.52 us
    unnamed x10, local copies, waits for them, and re-layouts  6.33 us
    pallas_call x1, Pallas kernels, local(): pl.pallas_call(local_kernel, out_shape=(jax.ShapeDtypeStruct((components,...  5.27 us
  transfers between devices with their start and end apart: 6, of which 4 were waited for; matrix products, arithmetic and copies ran while one was open for 0% of the time, Pallas kernels for 11%

profile of v3, /device:TPU:0, one launch (start us, length us, event | category | flops | bytes accessed | tf_op | source)
XLA Modules:
  0.0 105.8 jit_solution(7619424872927264084)
XLA Ops:
  0.6 0.0 copy-start.3
  0.6 2.8 %fusion = (bf16[128,2048]{1,0:T(8,128)(2,1)S(1)}, bf16[128,2048]{1,0:T(8,128)(2,1)}, bf16[128,2048]{1,0:T(8,128)(2,1)}, bf16[128,2048]{1,0:T(8,128)(2,1)S(1)}) fusion(bf16[256,8192]{1,0:T(8,128)(2,1)} %traffic_ref.1, s32[]{:T(128)S(6)} %select_n.3, s32[]{:T(128)S(6)} %add.6, s32[]{:T(128)S(6)} %add.5, s32[]{:T(128)S(6)} %add.4), kind=kLoop, calls=%fused_computation.2 | loop fusion | bytes 4194320 | tf_op jit(solution)/shard_map/split | solution.py:359
  3.5 3.0 %collective-permute-start.3 = (bf16[128,2048]{1,0:T(8,128)(2,1)S(1)}, bf16[128,2048]{1,0:T(8,128)(2,1)S(1)}, u32[]{:S(2)}, u32[]{:S(2)}) collective-permute-start(bf16[128,2048]{1,0:T(8,128)(2,1)S(1)} %get-tuple-element.26), channel_id=1, source_target_pairs={{0,1},{1,0},{2,3},{3,2},{4,5},{5,4},{6,7},{7,6},{8,9},{9,8},{10,11... | collective-permute-start | bytes 1572872 | tf_op jit(solution)/shard_map/ppermute | solution.py:359
  6.5 0.0 collective-permute-start.2
  6.5 2.0 %collective-permute-start.1 = (bf16[128,2048]{1,0:T(8,128)(2,1)}, bf16[128,2048]{1,0:T(8,128)(2,1)S(1)}, u32[]{:S(2)}, u32[]{:S(2)}) collective-permute-start(bf16[128,2048]{1,0:T(8,128)(2,1)} %get-tuple-element.28), channel_id=1, source_target_pairs={{0,1},{1,0},{2,3},{3,2},{4,5},{5,4},{6,7},{7,6},{8,9},{9,8},{10,11... | collective-permute-start | bytes 1572872 | tf_op jit(solution)/shard_map/ppermute | solution.py:359
  8.5 0.0 collective-permute-start
  8.5 0.0 copy-done.3
  8.5 5.3 %local.1 = (bf16[32,256,256]{2,1,0:T(8,128)(2,1)S(1)}, f32[384,128]{1,0:T(8,128)}) custom-call(bf16[256,8192]{1,0:T(8,128)(2,1)S(1)} %copy-done.3), custom_call_target="tpu_custom_call" | custom-call | flops 2147483648 | bytes 8388608 | tf_op jit(solution)/shard_map/local/pallas_call | solution.py:199
  13.8 0.0 copy-start
  13.8 1.9 %copy-done = bf16[32,256,256]{2,1,0:T(8,128)(2,1)} copy-done((bf16[32,256,256]{2,1,0:T(8,128)(2,1)}, bf16[32,256,256]{2,1,0:T(8,128)(2,1)S(1)}, u32[]{:S(2)}) %copy-start) | copy-done | bytes 4194328
  15.8 6.4 %all-to-all-start = ((f32[16,24,128]{2,1,0:T(8,128)}), f32[16,24,128]{2,1,0:T(8,128)S(1)}, u32[]{:S(2)}, u32[]{:S(2)}) async-start(f32[16,24,128]{2,1,0:T(8,128)} %bitcast), calls=%async_computation | async-start | bytes 393216 | tf_op jit(solution)/shard_map/all_to_all | solution.py:318
  22.2 0.0 collective-permute-done.3.traffic_ref
  22.2 0.0 copy-start.1
  22.2 2.2 %copy-done.1 = bf16[32,256,256]{2,1,0:T(8,128)(2,1)S(1)} copy-done((bf16[32,256,256]{2,1,0:T(8,128)(2,1)S(1)}, bf16[32,256,256]{2,1,0:T(8,128)(2,1)}, u32[]{:S(2)}) %copy-start.1) | copy-done | bytes 4194328
  24.4 1.4 %arrived.6 = (bf16[32,64,128]{2,1,0:T(8,128)(2,1)S(1)}, f32[64,256]{1,0:T(8,128)S(1)}) custom-call(s32[1]{0:T(128)} %bitcast.1.day_ref, bf16[128,2048]{1,0:T(8,128)(2,1)S(1)} %collective-permute-done.3.traffic_ref, bf16[32,256,256]{2,1,0:T(8,128)(2,1)S(1)} %copy-done.1), custom_call_target="tpu_custom_call" | custom-call | flops 268435456 | bytes 1048576 | tf_op jit(solution)/shard_map/arrived/pallas_call | solution.py:259
  25.8 4.7 %collective-permute-done.2.traffic_ref = bf16[128,2048]{1,0:T(8,128)(2,1)S(1)} collective-permute-done((bf16[128,2048]{1,0:T(8,128)(2,1)}, bf16[128,2048]{1,0:T(8,128)(2,1)S(1)}, u32[]{:S(2)}, u32[]{:S(2)}) %collective-permute-start.2) | collective-permute-done | bytes 524320 | tf_op jit(solution)/shard_map/ppermute | solution.py:359
  30.5 1.4 %arrived.5 = (bf16[32,64,128]{2,1,0:T(8,128)(2,1)S(1)}, f32[64,256]{1,0:T(8,128)S(1)}) custom-call(s32[1]{0:T(128)} %bitcast.1.day_ref, bf16[128,2048]{1,0:T(8,128)(2,1)S(1)} %collective-permute-done.2.traffic_ref, bf16[32,256,256]{2,1,0:T(8,128)(2,1)S(1)} %copy-done.1), custom_call_target="tpu_custom_call" | custom-call | flops 268435456 | bytes 1048576 | tf_op jit(solution)/shard_map/arrived/pallas_call | solution.py:259
  31.9 9.8 %collective-permute-done.1.traffic_ref = bf16[128,2048]{1,0:T(8,128)(2,1)S(1)} collective-permute-done((bf16[128,2048]{1,0:T(8,128)(2,1)}, bf16[128,2048]{1,0:T(8,128)(2,1)S(1)}, u32[]{:S(2)}, u32[]{:S(2)}) %collective-permute-start.1) | collective-permute-done | bytes 524320 | tf_op jit(solution)/shard_map/ppermute | solution.py:359
  41.7 1.4 %arrived.4 = (bf16[32,64,128]{2,1,0:T(8,128)(2,1)S(1)}, f32[64,256]{1,0:T(8,128)S(1)}) custom-call(s32[1]{0:T(128)} %bitcast.1.day_ref, bf16[128,2048]{1,0:T(8,128)(2,1)S(1)} %collective-permute-done.1.traffic_ref, bf16[32,256,256]{2,1,0:T(8,128)(2,1)S(1)} %copy-done.1), custom_call_target="tpu_custom_call" | custom-call | flops 268435456 | bytes 1048576 | tf_op jit(solution)/shard_map/arrived/pallas_call | solution.py:259
  43.2 0.0 copy-start.4
  43.2 8.9 %collective-permute-done.traffic_ref = bf16[128,2048]{1,0:T(8,128)(2,1)S(1)} collective-permute-done((bf16[128,2048]{1,0:T(8,128)(2,1)S(1)}, bf16[128,2048]{1,0:T(8,128)(2,1)S(1)}, u32[]{:S(2)}, u32[]{:S(2)}) %collective-permute-start) | collective-permute-done | bytes 524320 | tf_op jit(solution)/shard_map/ppermute | solution.py:359
  52.1 2.2 %arrived.7 = (bf16[32,64,128]{2,1,0:T(8,128)(2,1)S(1)}, f32[512,128]{1,0:T(8,128)}) custom-call(s32[1]{0:T(128)} %bitcast.1.day_ref, bf16[128,2048]{1,0:T(8,128)(2,1)S(1)} %collective-permute-done.traffic_ref, bf16[32,256,256]{2,1,0:T(8,128)(2,1)S(1)} %copy-done.1, f32[64,256]{1,0:T(8,128)S(1)} %get-tuple-element.16.refs_0_, ...), custom_call_target="tpu_custom_call" | custom-call | flops 268435456 | bytes 1048576 | tf_op jit(solution)/shard_map/arrived/pallas_call | solution.py:259
  54.3 0.0 all-to-all-done
  54.3 6.0 %all-to-all-start.1 = ((f32[32,16,128]{2,1,0:T(8,128)}), f32[32,16,128]{2,1,0:T(8,128)S(1)}, u32[]{:S(2)}, u32[]{:S(2)}) async-start(f32[32,16,128]{2,1,0:T(8,128)} %bitcast.2), calls=%async_computation.1 | async-start | bytes 524288 | tf_op jit(solution)/shard_map/all_to_all | solution.py:318
  60.4 10.6 %all-to-all-done.1 = f32[32,16,128]{2,1,0:T(8,128)S(1)} async-done(((f32[32,16,128]{2,1,0:T(8,128)}), f32[32,16,128]{2,1,0:T(8,128)S(1)}, u32[]{:S(2)}, u32[]{:S(2)}) %all-to-all-start.1) | async-done | bytes 262176 | tf_op jit(solution)/shard_map/all_to_all | solution.py:318
  71.1 19.9 %all_to_all.15.pieces_ref = f32[32,40,128]{2,1,0:T(8,128)S(1)} all-to-all(f32[32,40,128]{2,1,0:T(8,128)S(1)} %broadcast_in_dim.3), channel_id=1, replica_groups=mesh['sensor'=16,'day'=2] {'sensor','day'}, dimensions={0} | all-to-all | bytes 1310720 | tf_op jit(solution)/shard_map/all_to_all | solution.py:323
  91.0 0.0 copy-done.4
  91.0 10.6 %rounds.1 = (f32[64,512]{1,0:T(8,128)}, bf16[64,512]{1,0:T(8,128)(2,1)S(1)}) custom-call(f32[32,40,128]{2,1,0:T(8,128)S(1)} %all_to_all.15.pieces_ref, f32[64,512]{1,0:T(8,128)S(1)} %bitcast.5), custom_call_target="tpu_custom_call" | custom-call | tf_op jit(solution)/shard_map/rounds/pallas_call | solution.py:132
  101.7 0.0 copy-start.2
  101.7 2.2 %copy-done.2 = bf16[32,256,256]{2,1,0:T(8,128)(2,1)S(1)} copy-done((bf16[32,256,256]{2,1,0:T(8,128)(2,1)S(1)}, bf16[32,256,256]{2,1,0:T(8,128)(2,1)}, u32[]{:S(2)}) %copy-start.2) | copy-done | bytes 4194328
  103.8 2.0 %project.1 = bf16[128,2048]{1,0:T(8,128)(2,1)} custom-call(s32[1]{0:T(128)} %bitcast.1.day_ref, bf16[64,512]{1,0:T(8,128)(2,1)S(1)} %get-tuple-element.21.own_basis_ref.other_basis_ref, bf16[64,512]{1,0:T(8,128)(2,1)S(1)} %get-tuple-element.21.own_basis_ref.other_basis_ref, bf16[32,256,256]{2,1,0:T(8,128)(2,1)S(1)} %copy-done.2, ...), custom_call_target="tpu_custom_call" | custom-call | tf_op jit(solution)/shard_map/project/pallas_call | solution.py:306
  (4 shorter events, 0.1 us)
Async XLA Ops:
  0.6 7.9 %copy-start.3 = (bf16[256,8192]{1,0:T(8,128)(2,1)S(1)}, bf16[256,8192]{1,0:T(8,128)(2,1)}, u32[]{:S(2)}) copy-start(bf16[256,8192]{1,0:T(8,128)(2,1)} %traffic_ref.1) | copy-start | bytes 12582916
  3.5 18.7 %collective-permute-start.3 = (bf16[128,2048]{1,0:T(8,128)(2,1)S(1)}, bf16[128,2048]{1,0:T(8,128)(2,1)S(1)}, u32[]{:S(2)}, u32[]{:S(2)}) collective-permute-start(bf16[128,2048]{1,0:T(8,128)(2,1)S(1)} %get-tuple-element.26), channel_id=1, source_target_pairs={{0,1},{1,0},{2,3},{3,2},{4,5},{5,4},{6,7},{7,6},{8,9},{9,8},{10,11... | collective-permute-start | bytes 1572872 | tf_op jit(solution)/shard_map/ppermute | solution.py:359
  6.5 24.0 %collective-permute-start.2 = (bf16[128,2048]{1,0:T(8,128)(2,1)}, bf16[128,2048]{1,0:T(8,128)(2,1)S(1)}, u32[]{:S(2)}, u32[]{:S(2)}) collective-permute-start(bf16[128,2048]{1,0:T(8,128)(2,1)} %get-tuple-element.27), channel_id=1, source_target_pairs={{0,1},{1,0},{2,3},{3,2},{4,5},{5,4},{6,7},{7,6},{8,9},{9,8},{10,11... | collective-permute-start | bytes 1572872 | tf_op jit(solution)/shard_map/ppermute | solution.py:359
  6.5 35.2 %collective-permute-start.1 = (bf16[128,2048]{1,0:T(8,128)(2,1)}, bf16[128,2048]{1,0:T(8,128)(2,1)S(1)}, u32[]{:S(2)}, u32[]{:S(2)}) collective-permute-start(bf16[128,2048]{1,0:T(8,128)(2,1)} %get-tuple-element.28), channel_id=1, source_target_pairs={{0,1},{1,0},{2,3},{3,2},{4,5},{5,4},{6,7},{7,6},{8,9},{9,8},{10,11... | collective-permute-start | bytes 1572872 | tf_op jit(solution)/shard_map/ppermute | solution.py:359
  8.5 43.6 %collective-permute-start = (bf16[128,2048]{1,0:T(8,128)(2,1)S(1)}, bf16[128,2048]{1,0:T(8,128)(2,1)S(1)}, u32[]{:S(2)}, u32[]{:S(2)}) collective-permute-start(bf16[128,2048]{1,0:T(8,128)(2,1)S(1)} %get-tuple-element.29), channel_id=1, source_target_pairs={{0,1},{1,0},{2,3},{3,2},{4,5},{5,4},{6,7},{7,6},{8,9},{9,8},{10,11... | collective-permute-start | bytes 1572872 | tf_op jit(solution)/shard_map/ppermute | solution.py:359
  13.8 1.9 %copy-start = (bf16[32,256,256]{2,1,0:T(8,128)(2,1)}, bf16[32,256,256]{2,1,0:T(8,128)(2,1)S(1)}, u32[]{:S(2)}) copy-start(bf16[32,256,256]{2,1,0:T(8,128)(2,1)S(1)} %get-tuple-element.15.series_ref) | copy-start | bytes 12582916
  15.8 38.6 %all-to-all-start = ((f32[16,24,128]{2,1,0:T(8,128)}), f32[16,24,128]{2,1,0:T(8,128)S(1)}, u32[]{:S(2)}, u32[]{:S(2)}) async-start(f32[16,24,128]{2,1,0:T(8,128)} %bitcast), calls=%async_computation | async-start | bytes 393216 | tf_op jit(solution)/shard_map/all_to_all | solution.py:318
  22.2 2.2 %copy-start.1 = (bf16[32,256,256]{2,1,0:T(8,128)(2,1)S(1)}, bf16[32,256,256]{2,1,0:T(8,128)(2,1)}, u32[]{:S(2)}) copy-start(bf16[32,256,256]{2,1,0:T(8,128)(2,1)} %copy-done) | copy-start | bytes 12582916
  43.2 47.8 %copy-start.4 = (f32[512,64]{0,1:T(8,128)S(1)}, f32[512,64]{0,1:T(8,128)}, u32[]{:S(2)}) copy-start(f32[512,64]{0,1:T(8,128)} %param.3) | copy-start | bytes 393220
  54.3 16.7 %all-to-all-start.1 = ((f32[32,16,128]{2,1,0:T(8,128)}), f32[32,16,128]{2,1,0:T(8,128)S(1)}, u32[]{:S(2)}, u32[]{:S(2)}) async-start(f32[32,16,128]{2,1,0:T(8,128)} %bitcast.2), calls=%async_computation.1 | async-start | bytes 524288 | tf_op jit(solution)/shard_map/all_to_all | solution.py:318
  101.7 2.2 %copy-start.2 = (bf16[32,256,256]{2,1,0:T(8,128)(2,1)S(1)}, bf16[32,256,256]{2,1,0:T(8,128)(2,1)}, u32[]{:S(2)}) copy-start(bf16[32,256,256]{2,1,0:T(8,128)(2,1)} %copy-done) | copy-start | bytes 12582916

commit v4 on v3

--- a/solution.py
+++ b/solution.py
@@ -86,7 +86,7 @@
     finish(basis, day_basis_ref, low_ref)
 
 
-def pieces_rounds_kernel(sensor, own, pieces_ref, start_ref, day_basis_ref, low_ref, gram_ref):
+def join(sensor, own, pieces_ref, gram_ref):
     half = gram_ref.shape[0] // 2
     side = half // 2
     for day in range(2):
@@ -102,11 +102,47 @@
         block = off[part * half : (part + 1) * half]
         gram_ref[:half, half + part * side : half + (part + 1) * side] = block
         gram_ref[half + part * side : half + (part + 1) * side, :half] = block.T
+
+
+def finish_kernel(
+    own, count, day_ref, pieces_ref, start_ref, *refs
+):
+    series, (day_basis_ref, core_ref) = refs[: count + 1], refs[count + 1 : count + 3]
+    gram_ref, low_ref, own_ref, other_ref, done = refs[count + 3 :]
+    copies = [pltpu.make_async_copy(series[0], own_ref, done.at[0])]
+    at = 0
+    for k, part in enumerate(series[1:]):
+        here = part.shape[1]
+        copies.append(
+            pltpu.make_async_copy(part, other_ref.at[:, pl.ds(at, here), :], done.at[k + 1])
+        )
+        at += here
+    for copy in copies:
+        copy.start()
+    join(pieces_ref.shape[0] // 2, own, pieces_ref, gram_ref)
     basis = lax.fori_loop(0, ITERS, lambda _, b: one_round(gram_ref, b), start_ref[...])
     finish(basis, day_basis_ref, low_ref)
+    for copy in copies:
+        copy.wait()
+    components, days, _ = own_ref.shape
+    rank = low_ref.shape[0]
+    day = day_ref[0]
+    own_basis, other_basis = (
+        low_ref[:, pl.ds(pl.multiple_of(block * days, days), days)] for block in (day, 1 - day)
+    )
+    step = 128 // rank
+    for c in range(0, components, step):
+        values = []
+        for k in range(c, c + step):
+            both = jnp.dot(own_basis, own_ref[k], preferred_element_type=jnp.float32)
+            both += jnp.dot(other_basis, other_ref[k], preferred_element_type=jnp.float32)
+            values.append(both)
+        turned = jnp.concatenate(values, axis=0).T
+        core_ref[:, c * rank : (c + step) * rank] = turned.astype(jnp.bfloat16)
 
 
 WHOLE = pl.BlockSpec(memory_space=pltpu.VMEM)
+SCALAR = pl.BlockSpec(memory_space=pltpu.SMEM)
 VMEM_LIMIT = 24 * 1024 * 1024
 
 
@@ -127,17 +163,34 @@
     )(gram, start)
 
 
-def pieces_rounds(pieces, own, start):
-    days = start.shape[1]
+def finish_pairs(day, pieces, own, start, series, parts):
+    rank, days_all = start.shape
+    components, days, sensors = series.shape
+    anywhere = pl.BlockSpec(memory_space=pltpu.HBM)
+    regrouped = pltpu.VMEM((components, days, sensors), jnp.bfloat16)
     return pl.pallas_call(
-        functools.partial(pieces_rounds_kernel, pieces.shape[0] // 2, own),
-        out_shape=basis_shapes(start),
-        in_specs=[WHOLE, WHOLE],
+        functools.partial(finish_kernel, own, len(parts)),
+        out_shape=(
+            jax.ShapeDtypeStruct(start.shape, jnp.float32),
+            jax.ShapeDtypeStruct((sensors, components * rank), jnp.bfloat16),
+        ),
+        in_specs=[SCALAR, WHOLE, WHOLE, anywhere, *(anywhere for _ in parts)],
         out_specs=(WHOLE, WHOLE),
-        scratch_shapes=[pltpu.VMEM((days, days), jnp.float32)],
+        scratch_shapes=[
+            pltpu.VMEM((days_all, days_all), jnp.float32),
+            pltpu.VMEM(start.shape, jnp.bfloat16),
+            regrouped,
+            regrouped,
+            pltpu.SemaphoreType.DMA((len(parts) + 1,)),
+        ],
         compiler_params=pltpu.CompilerParams(vmem_limit_bytes=VMEM_LIMIT),
-        name="rounds",
-    )(pieces, start)
+        name="finish",
+    )(
+        day,
+        pieces,
+        start,
+        *(pltpu.with_memory_space_constraint(array, pltpu.HBM) for array in (series, *parts)),
+    )
 
 
 GROUP = 8
@@ -179,137 +232,84 @@
     return total
 
 
-def local_kernel(traffic_ref, series_ref, packed_ref):
-    components = series_ref.shape[0]
-
+def local_kernel(day_ref, traffic_ref, series_ref, packed_ref, all_ref):
     def put(day, values):
-        series_ref[:, day : day + values.shape[1], :] = values
-
-    components_first(traffic_ref, components, put)
-    gram = paired_dot(series_ref, series_ref)
+        all_ref[:, day : day + values.shape[1], :] = values
+
+    components_first(traffic_ref, all_ref.shape[0], put)
+    sensors = series_ref.shape[2]
+    series_ref[...] = all_ref[:, :, pl.ds(pl.multiple_of(day_ref[0] * sensors, sensors), sensors)]
+    gram = paired_dot(all_ref, all_ref)
     side = gram.shape[0] // 2
     packed_ref[:side] = gram[:side, :side]
     packed_ref[side : 2 * side] = gram[side:, :side]
     packed_ref[2 * side :] = gram[side:, side:]
 
 
-def local(traffic, days, components):
+def local(day, traffic, days, components):
     sensors = traffic.shape[0]
     side = days // 2
     return pl.pallas_call(
         local_kernel,
         out_shape=(
-            jax.ShapeDtypeStruct((components, days, sensors), jnp.bfloat16),
+            jax.ShapeDtypeStruct((components, days, sensors // 2), jnp.bfloat16),
             jax.ShapeDtypeStruct((3 * side, side), jnp.float32),
         ),
-        in_specs=[WHOLE],
+        in_specs=[SCALAR, WHOLE],
+        out_specs=(WHOLE, WHOLE),
+        scratch_shapes=[pltpu.VMEM((components, days, sensors), jnp.bfloat16)],
+        compiler_params=pltpu.CompilerParams(vmem_limit_bytes=VMEM_LIMIT),
+        cost_estimate=pl.CostEstimate(
+            flops=2 * traffic.size * (days + 256), bytes_accessed=4 * traffic.size, transcendentals=0
+        ),
+        name="local",
+    )(day, traffic)
+
+
+def arrived_kernel(first, day_ref, traffic_ref, series_ref, *refs):
+    arrived_ref, gram_ref = refs[-2:]
+    for before_ref in refs[:-2]:
+        gram_ref[...] = before_ref[...]
+
+    def put(day, values):
+        arrived_ref[:, day : day + values.shape[1], :] = values
+
+    components_first(traffic_ref, series_ref.shape[0], put)
+    here, days, side = arrived_ref.shape[1], series_ref.shape[1], gram_ref.shape[1]
+
+    @pl.when(day_ref[0] == 0)
+    def _():
+        gram = paired_dot(series_ref, arrived_ref)
+        row, lane = first // side * days, first % side
+        gram_ref[row : row + days, lane : lane + here] = gram
+
+    @pl.when(day_ref[0] != 0)
+    def _():
+        gram = paired_dot(arrived_ref, series_ref)
+        for part in range(days // side):
+            row = part * days + first
+            gram_ref[row : row + here, :] = gram[:, part * side : (part + 1) * side]
+
+
+def arrived(day, traffic, series, gram, first):
+    components, days, sensors = series.shape
+    here = traffic.shape[1] // components
+    side = days // 2
+    before = () if gram is None else (gram,)
+    return pl.pallas_call(
+        functools.partial(arrived_kernel, first),
+        out_shape=(
+            jax.ShapeDtypeStruct((components, here, sensors), jnp.bfloat16),
+            jax.ShapeDtypeStruct((2 * days, side), jnp.float32),
+        ),
+        in_specs=[SCALAR, WHOLE, WHOLE, *(WHOLE for _ in before)],
         out_specs=(WHOLE, WHOLE),
         compiler_params=pltpu.CompilerParams(vmem_limit_bytes=VMEM_LIMIT),
         cost_estimate=pl.CostEstimate(
             flops=2 * traffic.size * (days + 256), bytes_accessed=4 * traffic.size, transcendentals=0
         ),
-        name="local",
-    )(traffic)
-
-
-def arrived_kernel(before, day_ref, traffic_ref, series_ref, *refs):
-    parts, (arrived_ref, gram_ref) = refs[:before], refs[before:]
-
-    def put(day, values):
-        arrived_ref[:, day : day + values.shape[1], :] = values
-
-    components_first(traffic_ref, series_ref.shape[0], put)
-    gram = paired_dot(arrived_ref, series_ref)
-    if gram_ref.shape == gram.shape:
-        gram_ref[...] = gram
-        return
-    gram = jnp.concatenate([*(part[...] for part in parts), gram], axis=0)
-    side = gram_ref.shape[1]
-
-    @pl.when(day_ref[0] == 0)
-    def _():
-        turned = gram.T
-        gram_ref[: turned.shape[0]] = turned[:, :side]
-        gram_ref[turned.shape[0] :] = turned[:, side:]
-
-    @pl.when(day_ref[0] != 0)
-    def _():
-        gram_ref[: gram.shape[0]] = gram[:, :side]
-        gram_ref[gram.shape[0] :] = gram[:, side:]
-
-
-def arrived(day, traffic, series, parts, last):
-    components, days, _ = series.shape
-    sensors = traffic.shape[0]
-    here = traffic.shape[1] // components
-    gram_shape = (2 * days, days // 2) if last else (here, days)
-    grid_spec = pltpu.PrefetchScalarGridSpec(
-        num_scalar_prefetch=1,
-        grid=(1,),
-        in_specs=[
-            pl.BlockSpec(traffic.shape, lambda i, day: (0, 0)),
-            pl.BlockSpec((components, days, sensors), lambda i, day: (0, 0, day[0])),
-            *(pl.BlockSpec(part.shape, lambda i, day: (0, 0)) for part in parts),
-        ],
-        out_specs=(
-            pl.BlockSpec((components, here, sensors), lambda i, day: (0, 0, 0)),
-            pl.BlockSpec(gram_shape, lambda i, day: (0, 0)),
-        ),
-    )
-    return pl.pallas_call(
-        functools.partial(arrived_kernel, len(parts)),
-        grid_spec=grid_spec,
-        out_shape=(
-            jax.ShapeDtypeStruct((components, here, sensors), jnp.bfloat16),
-            jax.ShapeDtypeStruct(gram_shape, jnp.float32),
-        ),
-        compiler_params=pltpu.CompilerParams(vmem_limit_bytes=VMEM_LIMIT),
-        cost_estimate=pl.CostEstimate(
-            flops=2 * traffic.size * (days + 256), bytes_accessed=4 * traffic.size, transcendentals=0
-        ),
         name="arrived",
-    )(day, traffic, series, *parts)
-
-
-def project_kernel(day_ref, own_basis_ref, other_basis_ref, series_ref, *refs):
-    arrived_refs, core_ref = refs[:-1], refs[-1]
-    components = series_ref.shape[0]
-    rank = own_basis_ref.shape[0]
-
-    def column(c):
-        other = jnp.concatenate([ref[c] for ref in arrived_refs], axis=0)
-        values = jnp.dot(own_basis_ref[...], series_ref[c], preferred_element_type=jnp.float32)
-        values += jnp.dot(other_basis_ref[...], other, preferred_element_type=jnp.float32)
-        return values
-
-    step = 128 // rank
-    for c in range(0, components, step):
-        values = jnp.concatenate([column(c + k) for k in range(step)], axis=0)
-        core_ref[:, c * rank : (c + step) * rank] = values.T.astype(jnp.bfloat16)
-
-
-def project(day, basis, series, parts):
-    components, days, _ = series.shape
-    sensors = parts[0].shape[2]
-    rank = basis.shape[0]
-    grid_spec = pltpu.PrefetchScalarGridSpec(
-        num_scalar_prefetch=1,
-        grid=(1,),
-        in_specs=[
-            pl.BlockSpec((rank, days), lambda i, day: (0, day[0])),
-            pl.BlockSpec((rank, days), lambda i, day: (0, 1 - day[0])),
-            pl.BlockSpec((components, days, sensors), lambda i, day: (0, 0, day[0])),
-            *(pl.BlockSpec(part.shape, lambda i, day: (0, 0, 0)) for part in parts),
-        ],
-        out_specs=pl.BlockSpec((sensors, components * rank), lambda i, day: (0, 0)),
-    )
-    return pl.pallas_call(
-        project_kernel,
-        grid_spec=grid_spec,
-        out_shape=jax.ShapeDtypeStruct((sensors, components * rank), jnp.bfloat16),
-        compiler_params=pltpu.CompilerParams(vmem_limit_bytes=VMEM_LIMIT),
-        name="project",
-    )(day, basis, basis, series, *parts)
+    )(day, traffic, series, *before)
 
 
 def scatter_sum(values, axes):
@@ -353,24 +353,24 @@
     components = traffic.shape[1] // days
     sensors = traffic.shape[0] // 2
     day = lax.axis_index("day")
-    swap = [(0, 1), (1, 0)]
-    wanted = lax.dynamic_slice_in_dim(traffic, (1 - day) * sensors, sensors, axis=0)
-    chunks = [
-        lax.ppermute(chunk, "day", swap) for chunk in jnp.split(wanted, CHUNKS, axis=1)
-    ]
-    series, packed = local(traffic, days, components)
+    index = day.astype(jnp.int32).reshape(1)
+    wide = traffic.shape[1] // CHUNKS
+    row = (1 - day) * sensors
+    chunks = []
+    for at in range(CHUNKS):
+        wanted = lax.dynamic_slice(traffic, (row, at * wide), (sensors, wide))
+        if at == 0:
+            wanted, row = lax.optimization_barrier((wanted, row))
+        chunks.append(lax.ppermute(wanted, "day", [(0, 1), (1, 0)]))
+    series, packed = local(index, traffic, days, components)
     own = scatter_sum(packed, "sensor")
-    index = day.astype(jnp.int32).reshape(1)
-    parts, grams = [], []
+    parts, off = [], None
     for at, chunk in enumerate(chunks):
-        last = at == CHUNKS - 1
-        part, gram = arrived(index, chunk, series, grams if last else (), last)
+        part, off = arrived(index, chunk, series, off, at * days // CHUNKS)
         parts.append(part)
-        grams.append(gram)
-    off = scatter_sum(grams[-1], AXES)
-    pieces = gather(jnp.concatenate([own, off], axis=0), AXES)
-    day_basis, basis_low = pieces_rounds(pieces, own.shape[0], start_basis.T)
-    return (day_basis.T, project(index, basis_low, series, parts))
+    pieces = gather(jnp.concatenate([own, scatter_sum(off, AXES)], axis=0), AXES)
+    day_basis, core = finish_pairs(index, pieces, own.shape[0], start_basis.T, series, parts)
+    return (day_basis.T, core)
 
 
 def pairs(mesh):

time: 107 us -> 103 us (0.963)
  waiting for transfers between devices: 34.1 us -> 29.5 us
    dynamic_slice x0 -> x2, local copies, waits for them, and re-layouts: none -> 4.62 us  [paired_shards(): wanted = lax.dynamic_slice(traffic, (row, at * wide), (sensors, wide))]
    ppermute x4, waiting for transfers between devices: 23.4 us -> 18.8 us  [paired_shards(): chunks.append(lax.ppermute(wanted, 'day', [(0, 1), (1, 0)]))]
    split x1 -> x0, local copies, waits for them, and re-layouts: 2.84 us -> none  [paired_shards(): jnp.split(wanted, CHUNKS, axis=1)]
    unnamed x10 -> x14, local copies, waits for them, and re-layouts: 6.33 us -> 5.41 us
    pallas_call x6 -> x5, Pallas kernels: 19.2 us -> 19 us  [the longest x1 11.6 us: finish_pairs(): pl.pallas_call(functools.partial(finish_kernel, own, len(parts)), out_sha...]
  transfers between devices with their start and end apart: 6 -> 6, of which waited for: 4 -> 4; matrix products, arithmetic and copies ran while one was open for 0% -> 3% of each run, Pallas kernels for 11% -> 13%
where the time goes in v4:
time: 103 us
  waiting for transfers between devices  29.5 us (29%)
  Pallas kernels  24.6 us (24%)
  blocking collectives  19.9 us (19%)
  starting transfers between devices  17.6 us (17%)
  local copies, waits for them, and re-layouts  10.1 us (10%)
    all_to_all x1, blocking collectives, gather(): return lax.all_to_all(copies, axes, split_axis=0, concat_axis=0, tiled=True)  19.9 us
    ppermute x4, waiting for transfers between devices, paired_shards(): chunks.append(lax.ppermute(wanted, 'day', [(0, 1), (1, 0)]))  18.8 us
    all_to_all x2, starting transfers between devices, scatter_sum(): lax.all_to_all(pieces, axes, split_axis=0, concat_axis=0, tiled=True)  12.5 us
    pallas_call x1, Pallas kernels, finish_pairs(): pl.pallas_call(functools.partial(finish_kernel, own, len(parts)), out_sha...  11.6 us
    all_to_all x2, waiting for transfers between devices, scatter_sum(): lax.all_to_all(pieces, axes, split_axis=0, concat_axis=0, tiled=True)  10.6 us
    pallas_call x4, Pallas kernels, arrived(): pl.pallas_call(functools.partial(arrived_kernel, first), out_shape=(jax.S...  7.4 us
    pallas_call x1, Pallas kernels, local(): pl.pallas_call(local_kernel, out_shape=(jax.ShapeDtypeStruct((components,...  5.63 us
    unnamed x14, local copies, waits for them, and re-layouts  5.41 us
  transfers between devices with their start and end apart: 6, of which 4 were waited for; matrix products, arithmetic and copies ran while one was open for 3% of the time, Pallas kernels for 13%

profile of v4, /device:TPU:0, one launch (start us, length us, event | category | flops | bytes accessed | tf_op | source)
XLA Modules:
  0.0 102.6 jit_solution(7864844623384415111)
XLA Ops:
  0.6 1.9 %constant_dynamic-slice_fusion.3 = bf16[128,2048]{1,0:T(8,128)(2,1)} fusion(bf16[256,8192]{1,0:T(8,128)(2,1)} %traffic_ref.1, s32[]{:T(128)S(6)} %select_n.8), kind=kLoop, calls=%fused_computation.4 | loop fusion | bytes 1048580 | tf_op jit(solution)/shard_map/dynamic_slice | solution.py:361
  2.5 3.0 %collective-permute-start.3 = (bf16[128,2048]{1,0:T(8,128)(2,1)}, bf16[128,2048]{1,0:T(8,128)(2,1)S(1)}, u32[]{:S(2)}, u32[]{:S(2)}) collective-permute-start(bf16[128,2048]{1,0:T(8,128)(2,1)} %constant_dynamic-slice_fusion.3), channel_id=1, source_target_pairs={{0,1},{1,0},{2,3},{3,2},{4,5},{5,4},{6,7},{7,6},{8,9},{9,8},{10,11... | collective-permute-start | bytes 1572872 | tf_op jit(solution)/shard_map/ppermute | solution.py:364
  5.5 2.7 %constant_dynamic-slice_fusion = (bf16[128,2048]{1,0:T(8,128)(2,1)}, bf16[128,2048]{1,0:T(8,128)(2,1)}, bf16[128,2048]{1,0:T(8,128)(2,1)}) fusion(bf16[256,8192]{1,0:T(8,128)(2,1)} %traffic_ref.1, s32[]{:T(128)S(6)} %select_n.9), kind=kLoop, calls=%fused_computation.1 | loop fusion | bytes 3145732 | tf_op jit(solution)/shard_map/dynamic_slice | solution.py:361
  8.2 0.0 collective-permute-start.2
  8.3 2.0 %collective-permute-start.1 = (bf16[128,2048]{1,0:T(8,128)(2,1)}, bf16[128,2048]{1,0:T(8,128)(2,1)}, u32[]{:S(2)}, u32[]{:S(2)}) collective-permute-start(bf16[128,2048]{1,0:T(8,128)(2,1)} %get-tuple-element.32), channel_id=1, source_target_pairs={{0,1},{1,0},{2,3},{3,2},{4,5},{5,4},{6,7},{7,6},{8,9},{9,8},{10,11... | collective-permute-start | bytes 1572872 | tf_op jit(solution)/shard_map/ppermute | solution.py:364
  10.3 0.0 collective-permute-start
  10.3 0.0 copy-start.1
  10.3 2.2 %copy-done.1 = bf16[256,8192]{1,0:T(8,128)(2,1)S(1)} copy-done((bf16[256,8192]{1,0:T(8,128)(2,1)S(1)}, bf16[256,8192]{1,0:T(8,128)(2,1)}, u32[]{:S(2)}) %copy-start.1) | copy-done | bytes 4194328
  12.5 5.6 %local.1 = (bf16[32,256,128]{2,1,0:T(8,128)(2,1)S(1)}, f32[384,128]{1,0:T(8,128)}) custom-call(s32[1]{0:T(128)} %bitcast.day_ref, bf16[256,8192]{1,0:T(8,128)(2,1)S(1)} %copy-done.1), custom_call_target="tpu_custom_call" | custom-call | flops 2147483648 | bytes 8388608 | tf_op jit(solution)/shard_map/local/pallas_call | solution.py:252
  18.1 6.4 %all-to-all-start = ((f32[16,24,128]{2,1,0:T(8,128)}), f32[16,24,128]{2,1,0:T(8,128)S(1)}, u32[]{:S(2)}, u32[]{:S(2)}) async-start(f32[16,24,128]{2,1,0:T(8,128)} %bitcast.1), calls=%async_computation | async-start | bytes 393216 | tf_op jit(solution)/shard_map/all_to_all | solution.py:318
  24.6 0.0 collective-permute-done.3.traffic_ref
  24.6 1.1 %arrived.4 = (bf16[32,64,128]{2,1,0:T(8,128)(2,1)S(1)}, f32[512,128]{1,0:T(8,128)S(1)}) custom-call(s32[1]{0:T(128)} %bitcast.day_ref, bf16[128,2048]{1,0:T(8,128)(2,1)S(1)} %collective-permute-done.3.traffic_ref, bf16[32,256,128]{2,1,0:T(8,128)(2,1)S(1)} %get-tuple-element.18.series_ref.refs_0_), custom_call_target="tpu_custom_call" | custom-call | flops 268435456 | bytes 1048576 | tf_op jit(solution)/shard_map/arrived/pallas_call | solution.py:299
  25.7 0.0 copy-start.2
  25.7 0.8 copy-done.2
  26.5 3.4 %collective-permute-done.2.traffic_ref = bf16[128,2048]{1,0:T(8,128)(2,1)} collective-permute-done((bf16[128,2048]{1,0:T(8,128)(2,1)}, bf16[128,2048]{1,0:T(8,128)(2,1)}, u32[]{:S(2)}, u32[]{:S(2)}) %collective-permute-start.2) | collective-permute-done | bytes 524320 | tf_op jit(solution)/shard_map/ppermute | solution.py:364
  29.9 2.2 %arrived.5 = (bf16[32,64,128]{2,1,0:T(8,128)(2,1)S(1)}, f32[512,128]{1,0:T(8,128)S(1)}) custom-call(s32[1]{0:T(128)} %bitcast.day_ref, bf16[128,2048]{1,0:T(8,128)(2,1)} %collective-permute-done.2.traffic_ref, bf16[32,256,128]{2,1,0:T(8,128)(2,1)S(1)} %get-tuple-element.18.series_ref.refs_0_, f32[512,128]{1,0:T(8,128)S(1)} %get-tuple-element.20.refs_0_), custom_call_target="tpu_custom_call" | custom-call | flops 268435456 | bytes 1048576 | tf_op jit(solution)/shard_map/arrived/pallas_call | solution.py:299
  32.1 0.0 copy-start.3
  32.1 0.8 copy-done.3
  32.9 8.2 %collective-permute-done.1.traffic_ref = bf16[128,2048]{1,0:T(8,128)(2,1)} collective-permute-done((bf16[128,2048]{1,0:T(8,128)(2,1)}, bf16[128,2048]{1,0:T(8,128)(2,1)}, u32[]{:S(2)}, u32[]{:S(2)}) %collective-permute-start.1) | collective-permute-done | bytes 524320 | tf_op jit(solution)/shard_map/ppermute | solution.py:364
  41.1 2.2 %arrived.6 = (bf16[32,64,128]{2,1,0:T(8,128)(2,1)S(1)}, f32[512,128]{1,0:T(8,128)S(1)}) custom-call(s32[1]{0:T(128)} %bitcast.day_ref, bf16[128,2048]{1,0:T(8,128)(2,1)} %collective-permute-done.1.traffic_ref, bf16[32,256,128]{2,1,0:T(8,128)(2,1)S(1)} %get-tuple-element.18.series_ref.refs_0_, f32[512,128]{1,0:T(8,128)S(1)} %get-tuple-element.21.refs_0_), custom_call_target="tpu_custom_call" | custom-call | flops 268435456 | bytes 1048576 | tf_op jit(solution)/shard_map/arrived/pallas_call | solution.py:299
  43.3 0.0 copy-start.4
  43.3 0.8 copy-done.4
  44.1 7.3 %collective-permute-done.traffic_ref = bf16[128,2048]{1,0:T(8,128)(2,1)S(1)} collective-permute-done((bf16[128,2048]{1,0:T(8,128)(2,1)}, bf16[128,2048]{1,0:T(8,128)(2,1)S(1)}, u32[]{:S(2)}, u32[]{:S(2)}) %collective-permute-start) | collective-permute-done | bytes 524320 | tf_op jit(solution)/shard_map/ppermute | solution.py:364
  51.4 0.0 copy-done
  51.4 1.9 %arrived.7 = (bf16[32,64,128]{2,1,0:T(8,128)(2,1)S(1)}, f32[512,128]{1,0:T(8,128)}) custom-call(s32[1]{0:T(128)} %bitcast.day_ref, bf16[128,2048]{1,0:T(8,128)(2,1)S(1)} %collective-permute-done.traffic_ref, bf16[32,256,128]{2,1,0:T(8,128)(2,1)S(1)} %get-tuple-element.18.series_ref.refs_0_, f32[512,128]{1,0:T(8,128)S(1)} %get-tuple-element.22.refs_0_), custom_call_target="tpu_custom_call" | custom-call | flops 268435456 | bytes 1048576 | tf_op jit(solution)/shard_map/arrived/pallas_call | solution.py:299
  53.3 0.8 copy-done.5
  54.1 0.0 all-to-all-done
  54.1 6.1 %all-to-all-start.1 = ((f32[32,16,128]{2,1,0:T(8,128)}), f32[32,16,128]{2,1,0:T(8,128)S(1)}, u32[]{:S(2)}, u32[]{:S(2)}) async-start(f32[32,16,128]{2,1,0:T(8,128)} %bitcast.2), calls=%async_computation.1 | async-start | bytes 524288 | tf_op jit(solution)/shard_map/all_to_all | solution.py:318
  60.2 10.6 %all-to-all-done.1 = f32[32,16,128]{2,1,0:T(8,128)S(1)} async-done(((f32[32,16,128]{2,1,0:T(8,128)}), f32[32,16,128]{2,1,0:T(8,128)S(1)}, u32[]{:S(2)}, u32[]{:S(2)}) %all-to-all-start.1) | async-done | bytes 262176 | tf_op jit(solution)/shard_map/all_to_all | solution.py:318
  71.0 19.9 %all_to_all.15.pieces_ref = f32[32,40,128]{2,1,0:T(8,128)S(1)} all-to-all(f32[32,40,128]{2,1,0:T(8,128)S(1)} %broadcast_in_dim.3), channel_id=1, replica_groups=mesh['sensor'=16,'day'=2] {'sensor','day'}, dimensions={0} | all-to-all | bytes 1310720 | tf_op jit(solution)/shard_map/all_to_all | solution.py:323
  90.8 0.0 copy-done.6
  90.8 11.6 %finish.1 = (f32[64,512]{1,0:T(8,128)}, bf16[128,2048]{1,0:T(8,128)(2,1)}) custom-call(s32[1]{0:T(128)} %bitcast.day_ref, f32[32,40,128]{2,1,0:T(8,128)S(1)} %all_to_all.15.pieces_ref, f32[64,512]{1,0:T(8,128)S(1)} %bitcast.5, bf16[32,256,128]{2,1,0:T(8,128)(2,1)} %copy-done, bf16[32,64,128]{2,1,0:T(8,128)(2,1)} %copy-done.2, ...), custom_call_target="tpu_custom_call" | custom-call | tf_op jit(solution)/shard_map/finish/pallas_call | solution.py:171
  (7 shorter events, 0.1 us)
Async XLA Ops:
  2.5 22.0 %collective-permute-start.3 = (bf16[128,2048]{1,0:T(8,128)(2,1)}, bf16[128,2048]{1,0:T(8,128)(2,1)S(1)}, u32[]{:S(2)}, u32[]{:S(2)}) collective-permute-start(bf16[128,2048]{1,0:T(8,128)(2,1)} %constant_dynamic-slice_fusion.3), channel_id=1, source_target_pairs={{0,1},{1,0},{2,3},{3,2},{4,5},{5,4},{6,7},{7,6},{8,9},{9,8},{10,11... | collective-permute-start | bytes 1572872 | tf_op jit(solution)/shard_map/ppermute | solution.py:364
  8.2 21.6 %collective-permute-start.2 = (bf16[128,2048]{1,0:T(8,128)(2,1)}, bf16[128,2048]{1,0:T(8,128)(2,1)}, u32[]{:S(2)}, u32[]{:S(2)}) collective-permute-start(bf16[128,2048]{1,0:T(8,128)(2,1)} %get-tuple-element.30), channel_id=1, source_target_pairs={{0,1},{1,0},{2,3},{3,2},{4,5},{5,4},{6,7},{7,6},{8,9},{9,8},{10,11... | collective-permute-start | bytes 1572872 | tf_op jit(solution)/shard_map/ppermute | solution.py:364
  8.3 32.8 %collective-permute-start.1 = (bf16[128,2048]{1,0:T(8,128)(2,1)}, bf16[128,2048]{1,0:T(8,128)(2,1)}, u32[]{:S(2)}, u32[]{:S(2)}) collective-permute-start(bf16[128,2048]{1,0:T(8,128)(2,1)} %get-tuple-element.32), channel_id=1, source_target_pairs={{0,1},{1,0},{2,3},{3,2},{4,5},{5,4},{6,7},{7,6},{8,9},{9,8},{10,11... | collective-permute-start | bytes 1572872 | tf_op jit(solution)/shard_map/ppermute | solution.py:364
  10.3 41.1 %collective-permute-start = (bf16[128,2048]{1,0:T(8,128)(2,1)}, bf16[128,2048]{1,0:T(8,128)(2,1)S(1)}, u32[]{:S(2)}, u32[]{:S(2)}) collective-permute-start(bf16[128,2048]{1,0:T(8,128)(2,1)} %get-tuple-element.31), channel_id=1, source_target_pairs={{0,1},{1,0},{2,3},{3,2},{4,5},{5,4},{6,7},{7,6},{8,9},{9,8},{10,11... | collective-permute-start | bytes 1572872 | tf_op jit(solution)/shard_map/ppermute | solution.py:364
  10.3 2.2 %copy-start.1 = (bf16[256,8192]{1,0:T(8,128)(2,1)S(1)}, bf16[256,8192]{1,0:T(8,128)(2,1)}, u32[]{:S(2)}) copy-start(bf16[256,8192]{1,0:T(8,128)(2,1)} %traffic_ref.1) | copy-start | bytes 12582916
  18.1 33.2 %copy-start = (bf16[32,256,128]{2,1,0:T(8,128)(2,1)}, bf16[32,256,128]{2,1,0:T(8,128)(2,1)S(1)}, u32[]{:S(2)}) copy-start(bf16[32,256,128]{2,1,0:T(8,128)(2,1)S(1)} %get-tuple-element.18.series_ref.refs_0_) | copy-start | bytes 6291460
  18.1 35.9 %all-to-all-start = ((f32[16,24,128]{2,1,0:T(8,128)}), f32[16,24,128]{2,1,0:T(8,128)S(1)}, u32[]{:S(2)}, u32[]{:S(2)}) async-start(f32[16,24,128]{2,1,0:T(8,128)} %bitcast.1), calls=%async_computation | async-start | bytes 393216 | tf_op jit(solution)/shard_map/all_to_all | solution.py:318
  25.7 0.8 copy-start.2
  32.1 0.8 copy-start.3
  41.1 49.8 %copy-start.6 = (f32[512,64]{0,1:T(8,128)S(1)}, f32[512,64]{0,1:T(8,128)}, u32[]{:S(2)}) copy-start(f32[512,64]{0,1:T(8,128)} %param.3) | copy-start | bytes 393220
  43.3 0.8 copy-start.4
  53.3 0.8 copy-start.5
  54.1 16.8 %all-to-all-start.1 = ((f32[32,16,128]{2,1,0:T(8,128)}), f32[32,16,128]{2,1,0:T(8,128)S(1)}, u32[]{:S(2)}, u32[]{:S(2)}) async-start(f32[32,16,128]{2,1,0:T(8,128)} %bitcast.2), calls=%async_computation.1 | async-start | bytes 524288 | tf_op jit(solution)/shard_map/all_to_all | solution.py:318

commit v5 on v4

--- a/solution.py
+++ b/solution.py
@@ -143,6 +143,7 @@
 
 WHOLE = pl.BlockSpec(memory_space=pltpu.VMEM)
 SCALAR = pl.BlockSpec(memory_space=pltpu.SMEM)
+OUTSIDE = pl.BlockSpec(memory_space=pltpu.HBM)
 VMEM_LIMIT = 24 * 1024 * 1024
 
 
@@ -166,7 +167,6 @@
 def finish_pairs(day, pieces, own, start, series, parts):
     rank, days_all = start.shape
     components, days, sensors = series.shape
-    anywhere = pl.BlockSpec(memory_space=pltpu.HBM)
     regrouped = pltpu.VMEM((components, days, sensors), jnp.bfloat16)
     return pl.pallas_call(
         functools.partial(finish_kernel, own, len(parts)),
@@ -174,7 +174,7 @@
             jax.ShapeDtypeStruct(start.shape, jnp.float32),
             jax.ShapeDtypeStruct((sensors, components * rank), jnp.bfloat16),
         ),
-        in_specs=[SCALAR, WHOLE, WHOLE, anywhere, *(anywhere for _ in parts)],
+        in_specs=[SCALAR, WHOLE, WHOLE, OUTSIDE, *(OUTSIDE for _ in parts)],
         out_specs=(WHOLE, WHOLE),
         scratch_shapes=[
             pltpu.VMEM((days_all, days_all), jnp.float32),
@@ -267,14 +267,16 @@
 
 
 def arrived_kernel(first, day_ref, traffic_ref, series_ref, *refs):
-    arrived_ref, gram_ref = refs[-2:]
-    for before_ref in refs[:-2]:
+    out_ref, gram_ref, arrived_ref, done = refs[-4:]
+    for before_ref in refs[:-4]:
         gram_ref[...] = before_ref[...]
 
     def put(day, values):
         arrived_ref[:, day : day + values.shape[1], :] = values
 
     components_first(traffic_ref, series_ref.shape[0], put)
+    out = pltpu.make_async_copy(arrived_ref, out_ref, done)
+    out.start()
     here, days, side = arrived_ref.shape[1], series_ref.shape[1], gram_ref.shape[1]
 
     @pl.when(day_ref[0] == 0)
@@ -289,6 +291,8 @@
         for part in range(days // side):
             row = part * days + first
             gram_ref[row : row + here, :] = gram[:, part * side : (part + 1) * side]
+
+    out.wait()
 
 
 def arrived(day, traffic, series, gram, first):
@@ -299,11 +303,15 @@
     return pl.pallas_call(
         functools.partial(arrived_kernel, first),
         out_shape=(
-            jax.ShapeDtypeStruct((components, here, sensors), jnp.bfloat16),
+            pltpu.HBM((components, here, sensors), jnp.bfloat16),
             jax.ShapeDtypeStruct((2 * days, side), jnp.float32),
         ),
         in_specs=[SCALAR, WHOLE, WHOLE, *(WHOLE for _ in before)],
-        out_specs=(WHOLE, WHOLE),
+        out_specs=(OUTSIDE, WHOLE),
+        scratch_shapes=[
+            pltpu.VMEM((components, here, sensors), jnp.bfloat16),
+            pltpu.SemaphoreType.DMA,
+        ],
         compiler_params=pltpu.CompilerParams(vmem_limit_bytes=VMEM_LIMIT),
         cost_estimate=pl.CostEstimate(
             flops=2 * traffic.size * (days + 256), bytes_accessed=4 * traffic.size, transcendentals=0
@@ -345,6 +353,38 @@
     return (day_basis.T, core.reshape(sensors_here, components * basis_low.shape[0]))
 
 
+def cut_kernel(first, row_ref, traffic_ref, *refs):
+    outs, done = refs[:-1], refs[-1]
+    copies = []
+    at = first
+    for k, out in enumerate(outs):
+        sensors, wide = out.shape
+        rows = pl.ds(pl.multiple_of(row_ref[0] * sensors, sensors), sensors)
+        copies.append(
+            pltpu.make_async_copy(traffic_ref.at[rows, pl.ds(at, wide)], out, done.at[k])
+        )
+        at += wide
+    for copy in copies:
+        copy.start()
+    for copy in copies:
+        copy.wait()
+
+
+def cut(block, traffic, sensors, first, widths):
+    return pl.pallas_call(
+        functools.partial(cut_kernel, first),
+        out_shape=tuple(jax.ShapeDtypeStruct((sensors, wide), traffic.dtype) for wide in widths),
+        in_specs=[SCALAR, OUTSIDE],
+        out_specs=tuple(WHOLE for _ in widths),
+        scratch_shapes=[pltpu.SemaphoreType.DMA((len(widths),))],
+        compiler_params=pltpu.CompilerParams(vmem_limit_bytes=VMEM_LIMIT),
+        cost_estimate=pl.CostEstimate(
+            flops=0, bytes_accessed=4 * sensors * sum(widths), transcendentals=0
+        ),
+        name="cut",
+    )(block, pltpu.with_memory_space_constraint(traffic, pltpu.HBM))
+
+
 CHUNKS = 4
 
 
@@ -355,13 +395,10 @@
     day = lax.axis_index("day")
     index = day.astype(jnp.int32).reshape(1)
     wide = traffic.shape[1] // CHUNKS
-    row = (1 - day) * sensors
     chunks = []
-    for at in range(CHUNKS):
-        wanted = lax.dynamic_slice(traffic, (row, at * wide), (sensors, wide))
-        if at == 0:
-            wanted, row = lax.optimization_barrier((wanted, row))
-        chunks.append(lax.ppermute(wanted, "day", [(0, 1), (1, 0)]))
+    for first, count in ((0, 1), (1, CHUNKS - 1)):
+        for wanted in cut(1 - index, traffic, sensors, first * wide, [wide] * count):
+            chunks.append(lax.ppermute(wanted, "day", [(0, 1), (1, 0)]))
     series, packed = local(index, traffic, days, components)
     own = scatter_sum(packed, "sensor")
     parts, off = [], None

time: 103 us -> 102 us (level)
  local copies, waits for them, and re-layouts: 10.1 us -> 0.06 us
  Pallas kernels: 24.6 us -> 29.9 us
  waiting for transfers between devices: 29.5 us -> 32.6 us
    unnamed x14 -> x6, local copies, waits for them, and re-layouts: 5.41 us -> 0.01 us
    pallas_call x4 -> x6, Pallas kernels: 7.4 us -> 12.7 us  [the longest x4 8.92 us: arrived(): pl.pallas_call(functools.partial(arrived_kernel, first), out_shape=(pltpu...]
    dynamic_slice x2 -> x0, local copies, waits for them, and re-layouts: 4.62 us -> none  [paired_shards(): wanted = lax.dynamic_slice(traffic, (row, at * wide), (sensors, wide))]
    ppermute x4, waiting for transfers between devices: 18.8 us -> 21.9 us  [paired_shards(): chunks.append(lax.ppermute(wanted, 'day', [(0, 1), (1, 0)]))]
  transfers between devices with their start and end apart: 6 -> 6, of which waited for: 4 -> 4; matrix products, arithmetic and copies ran while one was open for 3% -> 0% of each run, Pallas kernels for 13% -> 17%
where the time goes in v5:
time: 102 us; the launch traced here: 101 us
  waiting for transfers between devices  32.6 us (32%)
  Pallas kernels  29.9 us (29%)
  blocking collectives  19.9 us (20%)
  starting transfers between devices  17.6 us (17%)
    ppermute x4, waiting for transfers between devices, paired_shards(): chunks.append(lax.ppermute(wanted, 'day', [(0, 1), (1, 0)]))  21.9 us
    all_to_all x1, blocking collectives, gather(): return lax.all_to_all(copies, axes, split_axis=0, concat_axis=0, tiled=True)  19.9 us
    all_to_all x2, starting transfers between devices, scatter_sum(): lax.all_to_all(pieces, axes, split_axis=0, concat_axis=0, tiled=True)  12.4 us
    pallas_call x1, Pallas kernels, finish_pairs(): pl.pallas_call(functools.partial(finish_kernel, own, len(parts)), out_sha...  11.6 us
    all_to_all x2, waiting for transfers between devices, scatter_sum(): lax.all_to_all(pieces, axes, split_axis=0, concat_axis=0, tiled=True)  10.6 us
    pallas_call x4, Pallas kernels, arrived(): pl.pallas_call(functools.partial(arrived_kernel, first), out_shape=(pltpu...  8.92 us
    pallas_call x1, Pallas kernels, local(): pl.pallas_call(local_kernel, out_shape=(jax.ShapeDtypeStruct((components,...  5.64 us
    ppermute x4, starting transfers between devices, paired_shards(): chunks.append(lax.ppermute(wanted, 'day', [(0, 1), (1, 0)]))  5.28 us
  transfers between devices with their start and end apart: 6, of which 4 were waited for; matrix products, arithmetic and copies ran while one was open for 0% of the time, Pallas kernels for 17%

profile of v5, /device:TPU:0, one launch (start us, length us, event | category | flops | bytes accessed | tf_op | source)
XLA Modules:
  0.0 100.9 jit_solution(12603822702195528722)
XLA Ops:
  0.6 0.0 copy-start.1
  0.6 1.2 %cut.3 = bf16[128,2048]{1,0:T(8,128)(2,1)S(1)} custom-call(s32[1]{0:T(128)S(6)} %sub.4.row_ref, bf16[256,8192]{1,0:T(8,128)(2,1)} %traffic_ref.5), custom_call_target="tpu_custom_call" | custom-call | bytes 1048576 | tf_op jit(solution)/shard_map/cut/pallas_call | solution.py:374
  1.9 3.1 %collective-permute-start.3 = (bf16[128,2048]{1,0:T(8,128)(2,1)S(1)}, bf16[128,2048]{1,0:T(8,128)(2,1)}, u32[]{:S(2)}, u32[]{:S(2)}) collective-permute-start(bf16[128,2048]{1,0:T(8,128)(2,1)S(1)} %cut.3), channel_id=1, source_target_pairs={{0,1},{1,0},{2,3},{3,2},{4,5},{5,4},{6,7},{7,6},{8,9},{9,8},{10,11... | collective-permute-start | bytes 1572872 | tf_op jit(solution)/shard_map/ppermute | solution.py:401
  4.9 2.5 %cut.2 = (bf16[128,2048]{1,0:T(8,128)(2,1)}, bf16[128,2048]{1,0:T(8,128)(2,1)}, bf16[128,2048]{1,0:T(8,128)(2,1)}) custom-call(s32[1]{0:T(128)S(6)} %sub.4.row_ref, bf16[256,8192]{1,0:T(8,128)(2,1)} %traffic_ref.5), custom_call_target="tpu_custom_call" | custom-call | bytes 3145728 | tf_op jit(solution)/shard_map/cut/pallas_call | solution.py:374
  7.5 0.2 collective-permute-start.2
  7.7 1.9 %collective-permute-start.1 = (bf16[128,2048]{1,0:T(8,128)(2,1)}, bf16[128,2048]{1,0:T(8,128)(2,1)}, u32[]{:S(2)}, u32[]{:S(2)}) collective-permute-start(bf16[128,2048]{1,0:T(8,128)(2,1)} %get-tuple-element.20), channel_id=1, source_target_pairs={{0,1},{1,0},{2,3},{3,2},{4,5},{5,4},{6,7},{7,6},{8,9},{9,8},{10,11... | collective-permute-start | bytes 1572872 | tf_op jit(solution)/shard_map/ppermute | solution.py:401
  9.6 0.1 collective-permute-start
  9.7 0.0 copy-done.1
  9.7 5.6 %local.1 = (bf16[32,256,128]{2,1,0:T(8,128)(2,1)S(1)}, f32[384,128]{1,0:T(8,128)}) custom-call(s32[1]{0:T(128)} %bitcast.day_ref, bf16[256,8192]{1,0:T(8,128)(2,1)S(1)} %copy-done.1), custom_call_target="tpu_custom_call" | custom-call | flops 2147483648 | bytes 8388608 | tf_op jit(solution)/shard_map/local/pallas_call | solution.py:252
  15.3 0.0 copy-start
  15.3 6.3 %all-to-all-start = ((f32[16,24,128]{2,1,0:T(8,128)}), f32[16,24,128]{2,1,0:T(8,128)S(1)}, u32[]{:S(2)}, u32[]{:S(2)}) async-start(f32[16,24,128]{2,1,0:T(8,128)} %bitcast.1), calls=%async_computation | async-start | bytes 393216 | tf_op jit(solution)/shard_map/all_to_all | solution.py:326
  21.6 0.0 collective-permute-done.3.traffic_ref
  21.6 2.3 %arrived.4 = (bf16[32,64,128]{2,1,0:T(8,128)(2,1)}, f32[512,128]{1,0:T(8,128)S(1)}) custom-call(s32[1]{0:T(128)} %bitcast.day_ref, bf16[128,2048]{1,0:T(8,128)(2,1)} %collective-permute-done.3.traffic_ref, bf16[32,256,128]{2,1,0:T(8,128)(2,1)S(1)} %get-tuple-element.19.series_ref.refs_0_), custom_call_target="tpu_custom_call" | custom-call | flops 268435456 | bytes 1048576 | tf_op jit(solution)/shard_map/arrived/pallas_call | solution.py:303
  24.0 5.1 %collective-permute-done.2.traffic_ref = bf16[128,2048]{1,0:T(8,128)(2,1)} collective-permute-done((bf16[128,2048]{1,0:T(8,128)(2,1)}, bf16[128,2048]{1,0:T(8,128)(2,1)}, u32[]{:S(2)}, u32[]{:S(2)}) %collective-permute-start.2) | collective-permute-done | bytes 524320 | tf_op jit(solution)/shard_map/ppermute | solution.py:401
  29.0 2.3 %arrived.5 = (bf16[32,64,128]{2,1,0:T(8,128)(2,1)}, f32[512,128]{1,0:T(8,128)S(1)}) custom-call(s32[1]{0:T(128)} %bitcast.day_ref, bf16[128,2048]{1,0:T(8,128)(2,1)} %collective-permute-done.2.traffic_ref, bf16[32,256,128]{2,1,0:T(8,128)(2,1)S(1)} %get-tuple-element.19.series_ref.refs_0_, f32[512,128]{1,0:T(8,128)S(1)} %get-tuple-element.22.refs_0_), custom_call_target="tpu_custom_call" | custom-call | flops 268435456 | bytes 1048576 | tf_op jit(solution)/shard_map/arrived/pallas_call | solution.py:303
  31.4 8.9 %collective-permute-done.1.traffic_ref = bf16[128,2048]{1,0:T(8,128)(2,1)} collective-permute-done((bf16[128,2048]{1,0:T(8,128)(2,1)}, bf16[128,2048]{1,0:T(8,128)(2,1)}, u32[]{:S(2)}, u32[]{:S(2)}) %collective-permute-start.1) | collective-permute-done | bytes 524320 | tf_op jit(solution)/shard_map/ppermute | solution.py:401
  40.3 0.0 copy-start.2
  40.3 2.3 %arrived.6 = (bf16[32,64,128]{2,1,0:T(8,128)(2,1)}, f32[512,128]{1,0:T(8,128)S(1)}) custom-call(s32[1]{0:T(128)} %bitcast.day_ref, bf16[128,2048]{1,0:T(8,128)(2,1)} %collective-permute-done.1.traffic_ref, bf16[32,256,128]{2,1,0:T(8,128)(2,1)S(1)} %get-tuple-element.19.series_ref.refs_0_, f32[512,128]{1,0:T(8,128)S(1)} %get-tuple-element.23.refs_0_), custom_call_target="tpu_custom_call" | custom-call | flops 268435456 | bytes 1048576 | tf_op jit(solution)/shard_map/arrived/pallas_call | solution.py:303
  42.6 7.9 %collective-permute-done.traffic_ref = bf16[128,2048]{1,0:T(8,128)(2,1)S(1)} collective-permute-done((bf16[128,2048]{1,0:T(8,128)(2,1)}, bf16[128,2048]{1,0:T(8,128)(2,1)S(1)}, u32[]{:S(2)}, u32[]{:S(2)}) %collective-permute-start) | collective-permute-done | bytes 524320 | tf_op jit(solution)/shard_map/ppermute | solution.py:401
  50.5 0.0 copy-done
  50.6 2.0 %arrived.7 = (bf16[32,64,128]{2,1,0:T(8,128)(2,1)}, f32[512,128]{1,0:T(8,128)}) custom-call(s32[1]{0:T(128)} %bitcast.day_ref, bf16[128,2048]{1,0:T(8,128)(2,1)S(1)} %collective-permute-done.traffic_ref, bf16[32,256,128]{2,1,0:T(8,128)(2,1)S(1)} %get-tuple-element.19.series_ref.refs_0_, f32[512,128]{1,0:T(8,128)S(1)} %get-tuple-element.24.refs_0_), custom_call_target="tpu_custom_call" | custom-call | flops 268435456 | bytes 1048576 | tf_op jit(solution)/shard_map/arrived/pallas_call | solution.py:303
  52.5 0.0 all-to-all-done
  52.5 6.1 %all-to-all-start.1 = ((f32[32,16,128]{2,1,0:T(8,128)}), f32[32,16,128]{2,1,0:T(8,128)S(1)}, u32[]{:S(2)}, u32[]{:S(2)}) async-start(f32[32,16,128]{2,1,0:T(8,128)} %bitcast.2), calls=%async_computation.1 | async-start | bytes 524288 | tf_op jit(solution)/shard_map/all_to_all | solution.py:326
  58.7 10.6 %all-to-all-done.1 = f32[32,16,128]{2,1,0:T(8,128)S(1)} async-done(((f32[32,16,128]{2,1,0:T(8,128)}), f32[32,16,128]{2,1,0:T(8,128)S(1)}, u32[]{:S(2)}, u32[]{:S(2)}) %all-to-all-start.1) | async-done | bytes 262176 | tf_op jit(solution)/shard_map/all_to_all | solution.py:326
  69.4 19.9 %all_to_all.15.pieces_ref = f32[32,40,128]{2,1,0:T(8,128)S(1)} all-to-all(f32[32,40,128]{2,1,0:T(8,128)S(1)} %broadcast_in_dim.3), channel_id=1, replica_groups=mesh['sensor'=16,'day'=2] {'sensor','day'}, dimensions={0} | all-to-all | bytes 1310720 | tf_op jit(solution)/shard_map/all_to_all | solution.py:331
  89.3 0.0 copy-done.2
  89.3 11.6 %finish.1 = (f32[64,512]{1,0:T(8,128)}, bf16[128,2048]{1,0:T(8,128)(2,1)}) custom-call(s32[1]{0:T(128)} %bitcast.day_ref, f32[32,40,128]{2,1,0:T(8,128)S(1)} %all_to_all.15.pieces_ref, f32[64,512]{1,0:T(8,128)S(1)} %bitcast.5, bf16[32,256,128]{2,1,0:T(8,128)(2,1)} %copy-done, bf16[32,64,128]{2,1,0:T(8,128)(2,1)} %get-tuple-element.26.refs_1_, ...), custom_call_target="tpu_custom_call" | custom-call | tf_op jit(solution)/shard_map/finish/pallas_call | solution.py:171
  (4 shorter events, 0.1 us)
Async XLA Ops:
  0.6 9.1 %copy-start.1 = (bf16[256,8192]{1,0:T(8,128)(2,1)S(1)}, bf16[256,8192]{1,0:T(8,128)(2,1)}, u32[]{:S(2)}) copy-start(bf16[256,8192]{1,0:T(8,128)(2,1)} %traffic_ref.5) | copy-start | bytes 12582916
  1.9 19.8 %collective-permute-start.3 = (bf16[128,2048]{1,0:T(8,128)(2,1)S(1)}, bf16[128,2048]{1,0:T(8,128)(2,1)}, u32[]{:S(2)}, u32[]{:S(2)}) collective-permute-start(bf16[128,2048]{1,0:T(8,128)(2,1)S(1)} %cut.3), channel_id=1, source_target_pairs={{0,1},{1,0},{2,3},{3,2},{4,5},{5,4},{6,7},{7,6},{8,9},{9,8},{10,11... | collective-permute-start | bytes 1572872 | tf_op jit(solution)/shard_map/ppermute | solution.py:401
  7.5 21.6 %collective-permute-start.2 = (bf16[128,2048]{1,0:T(8,128)(2,1)}, bf16[128,2048]{1,0:T(8,128)(2,1)}, u32[]{:S(2)}, u32[]{:S(2)}) collective-permute-start(bf16[128,2048]{1,0:T(8,128)(2,1)} %get-tuple-element.21), channel_id=1, source_target_pairs={{0,1},{1,0},{2,3},{3,2},{4,5},{5,4},{6,7},{7,6},{8,9},{9,8},{10,11... | collective-permute-start | bytes 1572872 | tf_op jit(solution)/shard_map/ppermute | solution.py:401
  7.7 32.6 %collective-permute-start.1 = (bf16[128,2048]{1,0:T(8,128)(2,1)}, bf16[128,2048]{1,0:T(8,128)(2,1)}, u32[]{:S(2)}, u32[]{:S(2)}) collective-permute-start(bf16[128,2048]{1,0:T(8,128)(2,1)} %get-tuple-element.20), channel_id=1, source_target_pairs={{0,1},{1,0},{2,3},{3,2},{4,5},{5,4},{6,7},{7,6},{8,9},{9,8},{10,11... | collective-permute-start | bytes 1572872 | tf_op jit(solution)/shard_map/ppermute | solution.py:401
  9.6 41.0 %collective-permute-start = (bf16[128,2048]{1,0:T(8,128)(2,1)}, bf16[128,2048]{1,0:T(8,128)(2,1)S(1)}, u32[]{:S(2)}, u32[]{:S(2)}) collective-permute-start(bf16[128,2048]{1,0:T(8,128)(2,1)} %get-tuple-element.18), channel_id=1, source_target_pairs={{0,1},{1,0},{2,3},{3,2},{4,5},{5,4},{6,7},{7,6},{8,9},{9,8},{10,11... | collective-permute-start | bytes 1572872 | tf_op jit(solution)/shard_map/ppermute | solution.py:401
  15.3 35.2 %copy-start = (bf16[32,256,128]{2,1,0:T(8,128)(2,1)}, bf16[32,256,128]{2,1,0:T(8,128)(2,1)S(1)}, u32[]{:S(2)}) copy-start(bf16[32,256,128]{2,1,0:T(8,128)(2,1)S(1)} %get-tuple-element.19.series_ref.refs_0_) | copy-start | bytes 6291460
  15.3 37.2 %all-to-all-start = ((f32[16,24,128]{2,1,0:T(8,128)}), f32[16,24,128]{2,1,0:T(8,128)S(1)}, u32[]{:S(2)}, u32[]{:S(2)}) async-start(f32[16,24,128]{2,1,0:T(8,128)} %bitcast.1), calls=%async_computation | async-start | bytes 393216 | tf_op jit(solution)/shard_map/all_to_all | solution.py:326
  40.3 49.0 %copy-start.2 = (f32[512,64]{0,1:T(8,128)S(1)}, f32[512,64]{0,1:T(8,128)}, u32[]{:S(2)}) copy-start(f32[512,64]{0,1:T(8,128)} %param.3) | copy-start | bytes 393220
  52.5 16.7 %all-to-all-start.1 = ((f32[32,16,128]{2,1,0:T(8,128)}), f32[32,16,128]{2,1,0:T(8,128)S(1)}, u32[]{:S(2)}, u32[]{:S(2)}) async-start(f32[32,16,128]{2,1,0:T(8,128)} %bitcast.2), calls=%async_computation.1 | async-start | bytes 524288 | tf_op jit(solution)/shard_map/all_to_all | solution.py:326
